TPU v7x, 256 devices: a whole 4x4x8 slice. The times are simulated.
256 devices in a mesh: blk: 64 (over y, z, x_lo), inner: 4 (over x_hi, core).
Axes of the slice: x: 4 (x_hi: 2, x_lo: 2; x = x_hi * 2 + x_lo), y: 4, z: 8, core: 2. Of those that a mesh axis runs over, the one named last changes fastest.
Arguments:
- density: float32 [512, 9, 128, 128], P(('blk', 'inner')), may hold values from -0.5 to 0.5
- block_cols: int32 [512, 9], P(('blk', 'inner')), may hold values from 0 to 511, as said below
- targets: int32 [512, 9, 9], P(('blk', 'inner')), may hold values from 0 to 9, as said below
Outputs:
- purified: float32 [512, 9, 128, 128], P(('blk', 'inner'))
Inputs may be any that keep to these rules, and one draw needn't show every extreme that they name: `block_cols`: strips are runs of 8 block rows. Slots 0 .. 2, 3 .. 5 and 6 .. 8 of row k hold 3 distinct columns each, ascending, from the strip before k's own (cyclically), k's own strip, and the strip after it (cyclically); the own group always contains column k. targets[k, s, t] is the slot u with block_cols[block_cols[k, s], u] == block_cols[k, t], or 9 where row block_cols[k, s] does not store that column.
All inputs are finite; a program needn't handle non-finite values.
Results may differ from a plain program's by a relative error of at most 0.0001.
Values sent between devices are 32-bit elements; how exact they have to be, the bound alone decides.
A program may use at most 128 MiB of HBM per device.

v0:
```python
import jax
import jax.numpy as jnp
from jax import lax
from jax.sharding import PartitionSpec as P


def shifted(value, axis, steps):
    count = lax.axis_size(axis)
    pairs = [(source, (source + steps) % count) for source in range(count)]
    return lax.ppermute(value, axis, pairs)


def shards(density, block_cols, targets):
    local_rows, slot_total, block_side, _ = density.shape
    per_strip = slot_total // 3
    position = lax.axis_index("blk")
    cycle_size = lax.axis_size("blk")
    strip_rows = local_rows * lax.axis_size("inner")

    def panel_lookup(offset, slot_low, slot_high):
        width = slot_high - slot_low
        cell_total = strip_rows * width
        first_slot = (offset + 1) * per_strip
        sources = density[:, first_slot : first_slot + per_strip]
        block_products = jnp.einsum(
            "kmab,ktac->kmtbc", sources, density, precision=lax.Precision.HIGHEST
        )
        first_row = (position + offset) % cycle_size * strip_rows
        destination_rows = block_cols[:, first_slot : first_slot + per_strip] - first_row
        dest_slots = targets[:, first_slot : first_slot + per_strip, :]
        local_slot = dest_slots - slot_low
        keep = (dest_slots < slot_total) & (local_slot >= 0) & (local_slot < width)
        cells = destination_rows[:, :, None] * width + local_slot
        cells = jnp.where(keep, cells, cell_total)
        panel = jnp.zeros((cell_total, block_side, block_side), jnp.float32)
        panel = panel.at[cells.reshape(-1)].add(
            block_products.reshape(-1, block_side, block_side), mode="drop"
        )
        return panel.reshape(strip_rows, width, block_side, block_side)

    upper_low, upper_high = (0, slot_total)
    lower_low, lower_upper_bound = (0, slot_total)
    upper = panel_lookup(1, upper_low, upper_high)
    lower = panel_lookup(-1, lower_low, lower_upper_bound)
    from_below = shifted(upper, "blk", 1)
    from_above = shifted(lower, "blk", -1)
    total = panel_lookup(0, 0, slot_total)
    total = total.at[:, upper_low:upper_high].add(from_below)
    total = total.at[:, lower_low:lower_upper_bound].add(from_above)
    square = lax.psum_scatter(total, "inner", scatter_dimension=0, tiled=True)
    return 2.0 * density - square


def solution(mesh):
    return jax.shard_map(
        shards,
        mesh=mesh,
        in_specs=(
            P(("blk", "inner"), None, None, None),
            P(("blk", "inner"), None),
            P(("blk", "inner"), None, None),
        ),
        out_specs=P(("blk", "inner"), None, None, None),
        check_vma=False,
    )
```

profile of v0, /device:TPU:1, one launch (start us, length us, event | category | flops | bytes accessed | tf_op | source)
XLA Modules:
  0.0 321.7 jit_solution(14225369256865449271)
XLA Ops:
  6.5 0.0 reduce-scatter.2.cloned.1.call-start
  6.5 0.9 subtract_multiply_fusion.1
  7.4 0.1 copy.17
  7.5 0.1 copy.13
  7.6 0.1 copy.21
  7.7 0.8 fusion.10
  8.5 0.1 reshape.194
  8.6 4.3 %convolution_bitcast_fusion.1 = f32[2,3,9,128,128]{3,4,1,2,0:T(8,128)S(1)} fusion(f32[2,9,128,128]{3,2,1,0:T(8,128)} %param.11), kind=kOutput, calls=%fused_computation.5 | convolution fusion | flops 1358954496 | bytes 5111808 | tf_op jit(solution)/shard_map/kmab,ktac->kmtbc/dot_general | solution.py:25
  12.9 3.0 copy.20
  15.9 2.7 broadcast.147.clone.2
  18.6 0.0 copy-start
  18.6 13.5 %scatter_fusion.1 = f32[72,128,128]{2,1,0:T(8,128)} fusion(f32[72,128,128]{2,1,0:T(8,128)} %broadcast.147.clone.2, s32[54]{0:T(128)S(1)} %fusion.13, f32[54,128,128]{2,1,0:T(8,128)} %bitcast.48), kind=kCustom, calls=%fused_computation.1 | custom fusion | flops 884736 | bytes 10617048 | tf_op jit(solution)/shard_map/scatter-add | solution.py:36
  32.1 2.0 collective-permute-start
  34.1 0.0 copy-done
  34.1 4.8 %convolution_bitcast_fusion = f32[2,3,9,128,128]{3,4,1,2,0:T(8,128)} fusion(f32[2,9,128,128]{3,2,1,0:T(8,128)S(1)} %copy-done), kind=kOutput, calls=%fused_computation.4 | convolution fusion | flops 1358954496 | bytes 5111808 | tf_op jit(solution)/shard_map/kmab,ktac->kmtbc/dot_general | solution.py:25
  38.9 0.1 reshape.197
  39.0 5.2 %copy.24 = f32[2,3,9,128,128]{4,3,2,1,0:T(8,128)} copy(f32[2,3,9,128,128]{3,4,1,2,0:T(8,128)} %convolution_bitcast_fusion) | data formatting | bytes 7077888 | tf_op jit(solution)/shard_map/kmab,ktac->kmtbc/transpose | solution.py:25
  44.2 2.8 broadcast.147.clone
  47.0 13.1 %scatter_fusion.2 = f32[72,128,128]{2,1,0:T(8,128)} fusion(f32[72,128,128]{2,1,0:T(8,128)} %broadcast.147.clone, s32[54]{0:T(128)S(1)} %fusion.14, f32[54,128,128]{2,1,0:T(8,128)} %bitcast.49), kind=kCustom, calls=%fused_computation.2 | custom fusion | flops 884736 | bytes 10617048 | tf_op jit(solution)/shard_map/scatter-add | solution.py:36
  60.1 8.3 %collective-permute-start.1 = (f32[8,9,128,128]{3,2,1,0:T(8,128)}, f32[8,9,128,128]{3,2,1,0:T(8,128)}, u32[]{:S(2)}, u32[]{:S(2)}) collective-permute-start(f32[8,9,128,128]{3,2,1,0:T(8,128)} %bitcast.46), channel_id=1, source_target_pairs={{0,252},{4,0},{8,4},{12,8},{16,12},{20,16},{24,20},{28,24},{32,28}... | collective-permute-start | bytes 14155784 | tf_op jit(solution)/shard_map/ppermute | solution.py:10
  68.4 0.1 reshape.191
  68.5 4.7 %convolution_bitcast_fusion.2 = f32[2,3,9,128,128]{3,4,1,2,0:T(8,128)} fusion(f32[2,9,128,128]{3,2,1,0:T(8,128)S(1)} %copy-done), kind=kOutput, calls=%fused_computation.6 | convolution fusion | flops 1358954496 | bytes 5111808 | tf_op jit(solution)/shard_map/kmab,ktac->kmtbc/dot_general | solution.py:25
  73.2 5.2 %copy.16 = f32[2,3,9,128,128]{4,3,2,1,0:T(8,128)} copy(f32[2,3,9,128,128]{3,4,1,2,0:T(8,128)} %convolution_bitcast_fusion.2) | data formatting | bytes 7077888 | tf_op jit(solution)/shard_map/kmab,ktac->kmtbc/transpose | solution.py:25
  78.4 2.7 broadcast.147.clone.1
  81.2 13.0 %scatter_fusion = f32[72,128,128]{2,1,0:T(8,128)} fusion(f32[72,128,128]{2,1,0:T(8,128)} %broadcast.147.clone.1, s32[54]{0:T(128)S(1)} %fusion.12, f32[54,128,128]{2,1,0:T(8,128)} %bitcast.47), kind=kCustom, calls=%fused_computation | custom fusion | flops 884736 | bytes 10617048 | tf_op jit(solution)/shard_map/scatter-add | solution.py:36
  94.2 141.8 %collective-permute-done = f32[8,9,128,128]{3,2,1,0:T(8,128)} collective-permute-done((f32[8,9,128,128]{3,2,1,0:T(8,128)}, f32[8,9,128,128]{3,2,1,0:T(8,128)}, u32[]{:S(2)}, u32[]{:S(2)}) %collective-permute-start) | collective-permute-done | bytes 4718624 | tf_op jit(solution)/shard_map/ppermute | solution.py:10
  236.0 7.0 %collective-permute-done.1 = f32[8,9,128,128]{3,2,1,0:T(8,128)} collective-permute-done((f32[8,9,128,128]{3,2,1,0:T(8,128)}, f32[8,9,128,128]{3,2,1,0:T(8,128)}, u32[]{:S(2)}, u32[]{:S(2)}) %collective-permute-start.1) | collective-permute-done | bytes 4718624 | tf_op jit(solution)/shard_map/ppermute | solution.py:10
  243.0 9.3 %add_add_fusion = f32[8,9,128,128]{3,2,1,0:T(8,128)} fusion(f32[8,9,128,128]{3,2,1,0:T(8,128)} %collective-permute-done.1, f32[8,9,128,128]{3,2,1,0:T(8,128)} %bitcast.44, f32[8,9,128,128]{3,2,1,0:T(8,128)} %collective-permute-done), kind=kLoop, calls=%fused_computation.3 | loop fusion | flops 2359296 | bytes 18874368 | tf_op jit(solution)/shard_map/add | solution.py:49
  252.3 0.0 reduce-scatter.2.cloned.1.call-update
  252.4 60.1 %reduce-scatter.2.cloned.1.call-done = f32[2,9,128,128]{3,2,1,0:T(8,128)} async-done(((f32[8,9,128,128]{3,2,1,0:T(8,128)}), f32[2,9,128,128]{3,2,1,0:T(8,128)}) %reduce-scatter.2.cloned.1.call-update) | async-done | bytes 1179664 | tf_op jit(solution)/shard_map/reduce_scatter | solution.py:50
  312.4 2.4 multiply_subtract_fusion
  (6 shorter events, 0.0 us)
Async XLA Ops:
  6.5 305.9 %reduce-scatter.2.cloned.1.call-start = ((), (), s32[]{:S(2)}) async-start(), calls=%async_computation.1 | async-start | bytes 5898240 | tf_op jit(solution)/shard_map/reduce_scatter | solution.py:50
  18.6 15.5 %copy-start = (f32[2,9,128,128]{3,2,1,0:T(8,128)S(1)}, f32[2,9,128,128]{3,2,1,0:T(8,128)}, u32[]{:S(2)}) copy-start(f32[2,9,128,128]{3,2,1,0:T(8,128)} %param.11) | copy-start | bytes 3538948
  32.1 203.9 %collective-permute-start = (f32[8,9,128,128]{3,2,1,0:T(8,128)}, f32[8,9,128,128]{3,2,1,0:T(8,128)}, u32[]{:S(2)}, u32[]{:S(2)}) collective-permute-start(f32[8,9,128,128]{3,2,1,0:T(8,128)} %bitcast.45), channel_id=1, source_target_pairs={{0,4},{4,8},{8,12},{12,16},{16,20},{20,24},{24,28},{28,32},{32,36}... | collective-permute-start | bytes 14155784 | tf_op jit(solution)/shard_map/ppermute | solution.py:10
  60.1 182.9 %collective-permute-start.1 = (f32[8,9,128,128]{3,2,1,0:T(8,128)}, f32[8,9,128,128]{3,2,1,0:T(8,128)}, u32[]{:S(2)}, u32[]{:S(2)}) collective-permute-start(f32[8,9,128,128]{3,2,1,0:T(8,128)} %bitcast.46), channel_id=1, source_target_pairs={{0,252},{4,0},{8,4},{12,8},{16,12},{20,16},{24,20},{28,24},{32,28}... | collective-permute-start | bytes 14155784 | tf_op jit(solution)/shard_map/ppermute | solution.py:10
Sparse Core Ops, SparseCore 0:
  252.5 59.8 reduce-scatter.1
where the time goes:
time: 322 us
  waiting for transfers between devices  209 us (65%)
  other arithmetic  53 us (16%)
  local copies, waits for them, and re-layouts  22.2 us (7%)
  matrix products  13.9 us (4%)
  between operations  13.4 us (4%)
  starting transfers between devices  10.3 us (3%)
    ppermute x2, waiting for transfers between devices, shifted(): return lax.ppermute(value, axis, pairs)  149 us
    reduce_scatter x1, waiting for transfers between devices, shards(): square = lax.psum_scatter(total, 'inner', scatter_dimension=0, tiled=True)  60.1 us
    scatter-add x3, other arithmetic, panel_lookup(): panel.at[cells.reshape(-1)]  39.6 us
    dot_general x3, matrix products, panel_lookup(): jnp.einsum('kmab,ktac->kmtbc', sources, density, precision=lax.Precision....  13.9 us
    transpose x3, local copies, waits for them, and re-layouts, panel_lookup(): jnp.einsum('kmab,ktac->kmtbc', sources, density, precision=lax.Precision....  13.3 us
    ppermute x2, starting transfers between devices, shifted(): return lax.ppermute(value, axis, pairs)  10.3 us
    add x1, other arithmetic, shards(): total = total.at[:, lower_low:lower_upper_bound].add(from_above)  9.34 us
    another operation x3, local copies, waits for them, and re-layouts  8.27 us
  transfers between devices with their start and end apart: 3, of which 3 were waited for; matrix products, arithmetic and copies ran while one was open for 16% of the time, Pallas kernels for 0%

commit v1 on v0

v1 whole, which is shorter than its diff:
```python
import functools

import jax
import jax.numpy as jnp
from jax import lax
from jax.experimental import pallas as pl
from jax.experimental.pallas import tpu as pltpu
from jax.sharding import PartitionSpec as P

MESH = pl.DeviceIdType.MESH
PER = 3
NZ = 9
HALF = 6
X = 4
ROWS = 2


def gather_kernel(
    den, cols, own1, far, side, zrow, table,
    side_s, side_r, far_s, far_r, z_s, z_r,
    mown_s, mown_r, mfar_s, mfar_r, mside_s, mside_r, mz_s, mz_r,
    cols_s, cols_r, local_s,
):
    blk = lax.axis_index("blk")
    inner = lax.axis_index("inner")
    strips = lax.axis_size("blk")
    parity = lax.rem(blk, 2)
    core = lax.rem(inner, 2)
    chip_x = 2 * (inner // 2) + parity

    def at_x(x):
        x = lax.rem(x, X)
        return (blk - parity + lax.rem(x, 2), 2 * (x // 2) + core)

    right, left = at_x(chip_x + 1), at_x(chip_x + X - 1)
    mirror = (blk, inner + 1 - 2 * core)
    z_to = (lax.rem(blk + strips + 2 - 4 * parity, strips), inner)
    z_from = (lax.rem(blk + strips - 2 + 4 * parity, strips), inner)

    def peer(offset, other):
        return (lax.rem(blk + offset + strips, strips), lax.rem(inner + other, 4))

    peers = [(o, i) for o in (-1, 0, 1) for i in range(4) if (o, i) != (0, 0)]
    barrier = pltpu.get_barrier_semaphore()
    for o, i in peers:
        pl.semaphore_signal(barrier, inc=1, device_id=peer(o, i), device_id_type=MESH)
    for device in (z_to, z_from):
        pl.semaphore_signal(barrier, inc=1, device_id=device, device_id_type=MESH)
    pl.semaphore_wait(barrier, len(peers) + 2)

    sent = []

    def send(src, dst, s, r, device):
        copy = pltpu.make_async_remote_copy(
            src_ref=src, dst_ref=dst, send_sem=s, recv_sem=r,
            device_id=device, device_id_type=MESH,
        )
        copy.start()
        sent.append(copy)

    def arrived(dst, r):
        pltpu.make_async_remote_copy(
            src_ref=dst, dst_ref=dst, send_sem=r, recv_sem=r,
            device_id=mirror, device_id_type=MESH,
        ).wait_recv()

    def groups(p):
        return (1, 2 * p, 2 - 2 * p)

    def slots(group):
        return pl.ds(PER * group, PER)

    mine = groups(parity)
    theirs = groups(1 - parity)
    z_place = (PER * parity, PER * (1 - parity))

    for n in range(6):
        g, row = n // 2, n % 2
        cut = slots(mine[g])
        for sd, device in ((0, right), (1, left)):
            send(den.at[row, cut], side.at[0, sd, row, cut],
                 side_s.at[sd, n], side_r.at[sd, n], device)
    for k, (o, i) in enumerate(peers):
        send(cols, table.at[1 - o, inner], cols_s.at[k], cols_r.at[1 - o, inner], peer(o, i))
    local = pltpu.make_async_copy(cols, table.at[1, inner], local_s)
    local.start()
    for n in range(6):
        g, row = n // 2, n % 2
        cut = slots(g)
        send(den.at[row, cut], own1.at[row, cut], mown_s.at[n], mown_r.at[n], mirror)

    def z_arrived(m):
        g, row, sd = m // 4, (m // 2) % 2, m % 2
        place = pl.ds(z_place[g], PER)
        arrived(zrow.at[0, sd, row, place], z_r.at[m])
        send(zrow.at[0, sd, row, place], zrow.at[1, sd, row, place],
             mz_s.at[m], mz_r.at[m], mirror)

    def far_arrived(j):
        for row in range(2):
            cut = slots(mine[j])
            arrived(far.at[0, row, cut], far_r.at[row, j])
            send(far.at[0, row, cut], far.at[1, row, cut],
                 mfar_s.at[row, j], mfar_r.at[row, j], mirror)

    for n in range(6):
        g, row = n // 2, n % 2
        cut = slots(theirs[g])
        for sd in range(2):
            arrived(side.at[0, sd, row, cut], side_r.at[sd, n])
            if g < 2:
                m = 2 * n + sd
                send(side.at[0, sd, row, cut],
                     zrow.at[0, sd, row, pl.ds(z_place[g], PER)],
                     z_s.at[m], z_r.at[m], z_to)
            if row == sd:
                send(side.at[0, sd, row, cut], far.at[0, row, cut],
                     far_s.at[row, g], far_r.at[row, g], (right, left)[sd])
            if g != 1:
                m = 2 * row + sd + (4 if g == 2 else 0)
                send(side.at[0, sd, row, cut], side.at[1, sd, row, cut],
                     mside_s.at[m], mside_r.at[m], mirror)
        if n >= 2:
            z_arrived(n - 2)
    far_arrived(0)
    z_arrived(4)
    z_arrived(5)
    far_arrived(1)
    z_arrived(6)
    z_arrived(7)
    far_arrived(2)

    for n in range(6):
        g, row = n // 2, n % 2
        arrived(own1.at[row, slots(g)], mown_r.at[n])
        arrived(far.at[1, row, slots(mine[g])], mfar_r.at[row, g])
        for sd in range(2):
            if g != 1:
                m = 2 * row + sd + (4 if g == 2 else 0)
                arrived(side.at[1, sd, row, slots(theirs[g])], mside_r.at[m])
            if g < 2:
                m = 2 * n + sd
                arrived(zrow.at[1, sd, row, pl.ds(z_place[g], PER)], mz_r.at[m])
    local.wait()
    for o, i in peers:
        other = lax.rem(inner + i, 4)
        arrived(table.at[1 + o, other], cols_r.at[1 + o, other])
    for copy in sent:
        copy.wait_send()


def gather(density, block_cols):
    rows, nz, b, _ = density.shape
    f32 = density.dtype
    dma = pltpu.SemaphoreType.DMA
    anywhere = pl.BlockSpec(memory_space=pl.ANY)
    return pl.pallas_call(
        gather_kernel,
        out_shape=(
            jax.ShapeDtypeStruct((rows, nz, b, b), f32),
            jax.ShapeDtypeStruct((2, rows, nz, b, b), f32),
            jax.ShapeDtypeStruct((2, 2, rows, nz, b, b), f32),
            jax.ShapeDtypeStruct((2, 2, rows, HALF, b, b), f32),
            jax.ShapeDtypeStruct((3, 4, rows, nz), jnp.int32),
        ),
        in_specs=[anywhere, anywhere],
        out_specs=(anywhere,) * 5,
        scratch_shapes=[
            dma((2, 6)), dma((2, 6)), dma((2, 3)), dma((2, 3)), dma((8,)), dma((8,)),
            dma((6,)), dma((6,)), dma((2, 3)), dma((2, 3)),
            dma((8,)), dma((8,)), dma((8,)), dma((8,)),
            dma((11,)), dma((3, 4)), dma,
        ],
        compiler_params=pltpu.CompilerParams(collective_id=0, has_side_effects=True),
    )(density, block_cols)


def product_kernel(
    where, table, den, own1, far, side, zrow, out,
    held, acc, sem,
):
    blk, inner = where[0], where[1]
    parity = lax.rem(blk, 2)
    chip_x = 2 * (inner // 2) + parity
    core = lax.rem(inner, 2)
    side_low = PER * parity
    z_low = PER * (1 - parity)

    def source(q):
        if q < 2:
            return den.at[q], held.at[q]
        if q < 4:
            return own1.at[q - 2], held.at[q]
        if q < 8:
            return far.at[(q - 4) // 2, q % 2], held.at[q]
        if q < 16:
            m = q - 8
            cut = pl.ds(side_low, HALF)
            return side.at[m // 4, (m // 2) % 2, m % 2, cut], held.at[q, cut]
        m = q - 16
        return zrow.at[m // 4, (m // 2) % 2, m % 2], held.at[q, pl.ds(z_low, HALF)]

    copies = [pltpu.make_async_copy(*source(q), sem.at[q]) for q in range(24)]
    for copy in copies:
        copy.start()
    acc[...] = jnp.zeros_like(acc)

    def split(value):
        high = value.astype(jnp.bfloat16)
        return high, (value - high.astype(jnp.float32)).astype(jnp.bfloat16)

    def row_products(q, offset, owner, row, first, count):
        group = 2 - offset
        for mine in range(ROWS):
            me = blk * (4 * ROWS) + inner * ROWS + mine
            slot = jnp.int32(-1)
            for a in range(PER):
                s = PER * group + a
                slot = jnp.where(table[offset, owner, row, s] == me, s, slot)

            @pl.when(slot >= 0)
            def _():
                left = held[q, slot].T
                left_high, left_low = split(left)
                lhs = jnp.concatenate([left_high, left_low, left_high], axis=1)
                for t in range(count):
                    right_high, right_low = split(held[q, first + t])
                    rhs = jnp.concatenate([right_high, right_high, right_low], axis=0)
                    product = jnp.dot(lhs, rhs, preferred_element_type=jnp.float32)
                    e = offset - 1 + (first + t) // PER
                    column = table[offset, owner, row, first + t]
                    place = jnp.int32(NZ)
                    for a in range(PER):
                        u = PER * e + a
                        place = jnp.where(table[1, inner, mine, u] == column, u, place)
                    acc[mine, place] += product

    for q in range(24):
        copies[q].wait()
        row = q % 2
        if q < 8:
            owner = (inner, inner + 1 - 2 * core, lax.rem(inner + 2, 4),
                     lax.rem(inner + 2, 4) + 1 - 2 * core)[q // 2]
            row_products(q, 1, owner, row, 0, NZ)
        else:
            m = (q - 8) % 8
            half, sd = m // 4, (m // 2) % 2
            x = lax.rem(chip_x + (X - 1 if sd == 0 else 1), X)
            owner = 2 * (x // 2) + (core if half == 0 else 1 - core)
            if q < 16:
                row_products(q, 2 - 2 * parity, owner, row, side_low, HALF)
            else:
                row_products(q, 2 * parity, owner, row, z_low, HALF)
    out[...] = 2.0 * held[0:ROWS] - acc[:, 0:NZ]


def products(where, table, density, own1, far, side, zrow):
    rows, nz, b, _ = density.shape
    anywhere = pl.BlockSpec(memory_space=pl.ANY)
    return pl.pallas_call(
        product_kernel,
        out_shape=jax.ShapeDtypeStruct(density.shape, density.dtype),
        grid_spec=pltpu.PrefetchScalarGridSpec(
            num_scalar_prefetch=2,
            grid=(),
            in_specs=[anywhere] * 5,
            out_specs=pl.BlockSpec(memory_space=pltpu.VMEM),
            scratch_shapes=[
                pltpu.VMEM((24, nz, b, b), density.dtype),
                pltpu.VMEM((rows, nz + 1, b, b), density.dtype),
                pltpu.SemaphoreType.DMA((24,)),
            ],
        ),
        compiler_params=pltpu.CompilerParams(vmem_limit_bytes=40 * 2**20),
    )(where, table, density, own1, far, side, zrow)


def shards(density, block_cols, targets):
    del targets
    own1, far, side, zrow, table = gather(density, block_cols)
    where = jnp.stack([lax.axis_index("blk"), lax.axis_index("inner")]).astype(jnp.int32)
    return products(where, table, density, own1, far, side, zrow)


def solution(mesh):
    return jax.shard_map(
        shards,
        mesh=mesh,
        in_specs=(
            P(("blk", "inner"), None, None, None),
            P(("blk", "inner"), None),
            P(("blk", "inner"), None, None),
        ),
        out_specs=P(("blk", "inner"), None, None, None),
        check_vma=False,
    )
```

time: 322 us -> 79.7 us (0.25)
  waiting for transfers between devices: 209 us -> 0 us
  Pallas kernels: 0 us -> 69.8 us
  other arithmetic: 53 us -> 0.07 us
  matrix products: 13.9 us -> 0 us
  between operations: 13.4 us -> 0.18 us
  local copies, waits for them, and re-layouts: 22.2 us -> 9.13 us
  starting transfers between devices: 10.3 us -> 0 us
    ppermute x2 -> x0, waiting for transfers between devices: 149 us -> none  [shifted(): return lax.ppermute(value, axis, pairs)]
    pallas_call x0 -> x2, Pallas kernels: none -> 69.8 us  [the longest x1 57.2 us: gather(): pl.pallas_call(gather_kernel, out_shape=(jax.ShapeDtypeStruct((rows, nz,...]
    reduce_scatter x1 -> x0, waiting for transfers between devices: 60.1 us -> none  [shards(): square = lax.psum_scatter(total, 'inner', scatter_dimension=0, tiled=True)]
    scatter-add x3 -> x0, other arithmetic: 39.6 us -> none  [panel_lookup(): panel.at[cells.reshape(-1)]]
    dot_general x3 -> x0, matrix products: 13.9 us -> none  [panel_lookup(): jnp.einsum('kmab,ktac->kmtbc', sources, density, precision=lax.Precision....]
    transpose x3 -> x0, local copies, waits for them, and re-layouts: 13.3 us -> none  [panel_lookup(): jnp.einsum('kmab,ktac->kmtbc', sources, density, precision=lax.Precision....]
    ppermute x2 -> x0, starting transfers between devices: 10.3 us -> none  [shifted(): return lax.ppermute(value, axis, pairs)]
    add x1 -> x0, other arithmetic: 9.34 us -> none  [shards(): total = total.at[:, lower_low:lower_upper_bound].add(from_above)]
  transfers between devices with their start and end apart: 3 -> 0, of which waited for: 3 -> 0; matrix products, arithmetic and copies ran while one was open for 16% -> 0% of each run, Pallas kernels for 0% -> 0%
where the time goes in v1:
time: 79.7 us; the launch traced here: 79.2 us
  Pallas kernels  69.8 us (88%)
  local copies, waits for them, and re-layouts  9.13 us (11%)
    pallas_call x1, Pallas kernels, gather(): pl.pallas_call(gather_kernel, out_shape=(jax.ShapeDtypeStruct((rows, nz,...  57.2 us
    pallas_call x1, Pallas kernels, products(): pl.pallas_call(product_kernel, out_shape=jax.ShapeDtypeStruct(density.sha...  12.6 us
    unnamed x12, local copies, waits for them, and re-layouts  9.13 us

profile of v1, /device:TPU:1, one launch (start us, length us, event | category | flops | bytes accessed | tf_op | source)
XLA Modules:
  0.0 79.2 jit_solution(3618339557594387939)
XLA Ops:
  0.0 0.1 pad_add_fusion.where
  0.1 57.2 %shard_map.28 = (f32[2,9,128,128]{3,2,1,0:T(8,128)}, f32[2,2,9,128,128]{4,3,2,1,0:T(8,128)}, f32[2,2,2,9,128,128]{5,4,3,2,1,0:T(8,128)}, f32[2,2,2,6,128,128]{5,4,3,2,1,0:T(8,128)}, s32[3,4,2,9]{3,2,1,0:T(2,128)}) custom-call(f32[2,9,128,128]{3,2,1,0:T(8,128)} %den.3, s32[2,9]{1,0:T(2,128)} %cols.1), custom_call_target="tpu_custom_call" | custom-call | tf_op jit(solution)/shard_map/pallas_call | solution.py:157
  57.3 0.0 copy-start
  57.3 1.3 %copy-done = f32[2,9,128,128]{3,2,1,0:T(8,128)S(1)} copy-done((f32[2,9,128,128]{3,2,1,0:T(8,128)S(1)}, f32[2,9,128,128]{3,2,1,0:T(8,128)}, u32[]{:S(2)}) %copy-start) | copy-done | bytes 1179672
  58.6 0.0 copy-start.1
  58.6 2.3 %copy-done.1 = f32[2,2,2,9,128,128]{5,4,3,2,1,0:T(8,128)S(1)} copy-done((f32[2,2,2,9,128,128]{5,4,3,2,1,0:T(8,128)S(1)}, f32[2,2,2,9,128,128]{5,4,3,2,1,0:T(8,128)}, u32[]{:S(2)}) %copy-start.1) | copy-done | bytes 4718616
  60.9 0.0 copy-start.2
  60.9 1.9 %copy-done.2 = f32[2,2,2,6,128,128]{5,4,3,2,1,0:T(8,128)S(1)} copy-done((f32[2,2,2,6,128,128]{5,4,3,2,1,0:T(8,128)S(1)}, f32[2,2,2,6,128,128]{5,4,3,2,1,0:T(8,128)}, u32[]{:S(2)}) %copy-start.2) | copy-done | bytes 3145752
  62.8 0.0 copy-start.3
  62.8 1.7 %copy-done.3 = f32[2,2,9,128,128]{4,3,2,1,0:T(8,128)S(1)} copy-done((f32[2,2,9,128,128]{4,3,2,1,0:T(8,128)S(1)}, f32[2,2,9,128,128]{4,3,2,1,0:T(8,128)}, u32[]{:S(2)}) %copy-start.3) | copy-done | bytes 2359320
  64.5 0.0 copy-start.4
  64.5 1.3 %copy-done.4 = f32[2,9,128,128]{3,2,1,0:T(8,128)S(1)} copy-done((f32[2,9,128,128]{3,2,1,0:T(8,128)S(1)}, f32[2,9,128,128]{3,2,1,0:T(8,128)}, u32[]{:S(2)}) %copy-start.4) | copy-done | bytes 1179672
  65.7 0.0 copy-start.5
  65.7 0.7 copy-done.5
  66.5 12.6 %shard_map.29 = f32[2,9,128,128]{3,2,1,0:T(8,128)} custom-call(s32[2]{0:T(128)S(1)} %pad_add_fusion.where, s32[3,4,2,9]{3,2,1,0:T(2,128)S(1)} %copy-done.5, f32[2,9,128,128]{3,2,1,0:T(8,128)S(1)} %copy-done, f32[2,9,128,128]{3,2,1,0:T(8,128)S(1)} %copy-done.4, f32[2,2,9,128,128]{4,3,2,1,0:T(8,128)S(1)} %copy-done.3, ...), custom_call_target="tpu_custom_call" | custom-call | tf_op jit(solution)/shard_map/pallas_call | solution.py:260
Async XLA Ops:
  57.3 1.3 %copy-start = (f32[2,9,128,128]{3,2,1,0:T(8,128)S(1)}, f32[2,9,128,128]{3,2,1,0:T(8,128)}, u32[]{:S(2)}) copy-start(f32[2,9,128,128]{3,2,1,0:T(8,128)} %den.3) | copy-start | bytes 3538948
  58.6 2.3 %copy-start.1 = (f32[2,2,2,9,128,128]{5,4,3,2,1,0:T(8,128)S(1)}, f32[2,2,2,9,128,128]{5,4,3,2,1,0:T(8,128)}, u32[]{:S(2)}) copy-start(f32[2,2,2,9,128,128]{5,4,3,2,1,0:T(8,128)} %get-tuple-element.13.side) | copy-start | bytes 14155780
  60.9 1.9 %copy-start.2 = (f32[2,2,2,6,128,128]{5,4,3,2,1,0:T(8,128)S(1)}, f32[2,2,2,6,128,128]{5,4,3,2,1,0:T(8,128)}, u32[]{:S(2)}) copy-start(f32[2,2,2,6,128,128]{5,4,3,2,1,0:T(8,128)} %get-tuple-element.14.zrow) | copy-start | bytes 9437188
  62.8 1.7 %copy-start.3 = (f32[2,2,9,128,128]{4,3,2,1,0:T(8,128)S(1)}, f32[2,2,9,128,128]{4,3,2,1,0:T(8,128)}, u32[]{:S(2)}) copy-start(f32[2,2,9,128,128]{4,3,2,1,0:T(8,128)} %get-tuple-element.12.far) | copy-start | bytes 7077892
  64.5 1.3 %copy-start.4 = (f32[2,9,128,128]{3,2,1,0:T(8,128)S(1)}, f32[2,9,128,128]{3,2,1,0:T(8,128)}, u32[]{:S(2)}) copy-start(f32[2,9,128,128]{3,2,1,0:T(8,128)} %get-tuple-element.11.own1) | copy-start | bytes 3538948
  65.7 0.7 copy-start.5

commit v2 on v1

--- a/solution.py
+++ b/solution.py
@@ -271,7 +271,7 @@
                 pltpu.SemaphoreType.DMA((24,)),
             ],
         ),
-        compiler_params=pltpu.CompilerParams(vmem_limit_bytes=40 * 2**20),
+        compiler_params=pltpu.CompilerParams(vmem_limit_bytes=62 * 2**20),
     )(where, table, density, own1, far, side, zrow)
 
 

time: 79.7 us -> 70.7 us (0.89)
  local copies, waits for them, and re-layouts: 9.13 us -> 0 us
  Pallas kernels: 69.8 us -> 69 us
    unnamed x12 -> x0, local copies, waits for them, and re-layouts: 9.13 us -> none
where the time goes in v2:
time: 70.7 us; the launch traced here: 69.9 us
  Pallas kernels  69 us (98%)
    pallas_call x1, Pallas kernels, gather(): pl.pallas_call(gather_kernel, out_shape=(jax.ShapeDtypeStruct((rows, nz,...  57.1 us
    pallas_call x1, Pallas kernels, products(): pl.pallas_call(product_kernel, out_shape=jax.ShapeDtypeStruct(density.sha...  12 us

profile of v2, /device:TPU:1, one launch (start us, length us, event | category | flops | bytes accessed | tf_op | source)
XLA Modules:
  0.0 69.9 jit_solution(1905037824595657692)
XLA Ops:
  0.0 0.7 pad_add_fusion.where
  0.7 57.1 %shard_map.28 = (f32[2,9,128,128]{3,2,1,0:T(8,128)}, f32[2,2,9,128,128]{4,3,2,1,0:T(8,128)}, f32[2,2,2,9,128,128]{5,4,3,2,1,0:T(8,128)}, f32[2,2,2,6,128,128]{5,4,3,2,1,0:T(8,128)}, s32[3,4,2,9]{3,2,1,0:T(2,128)}) custom-call(f32[2,9,128,128]{3,2,1,0:T(8,128)} %den.3, s32[2,9]{1,0:T(2,128)} %cols.1), custom_call_target="tpu_custom_call" | custom-call | tf_op jit(solution)/shard_map/pallas_call | solution.py:157
  57.7 12.0 %shard_map.29 = f32[2,9,128,128]{3,2,1,0:T(8,128)} custom-call(s32[2]{0:T(128)} %pad_add_fusion.where, s32[3,4,2,9]{3,2,1,0:T(2,128)} %get-tuple-element.10.table, f32[2,9,128,128]{3,2,1,0:T(8,128)} %den.3, f32[2,9,128,128]{3,2,1,0:T(8,128)} %get-tuple-element.11.own1, f32[2,2,9,128,128]{4,3,2,1,0:T(8,128)} %get-tuple-element.12.far, ...), custom_call_target="tpu_custom_call" | custom-call | tf_op jit(solution)/shard_map/pallas_call | solution.py:260

commit v3 on v0

v3 whole, which is shorter than its diff:
```python
import jax
import jax.numpy as jnp
from jax import lax
from jax.experimental import pallas as pl
from jax.experimental.pallas import tpu as pltpu
from jax.sharding import PartitionSpec as P

MESH = pl.DeviceIdType.MESH
PER = 3
NZ = 9
X = 4
ROWS = 2


def split(value):
    high = value.astype(jnp.bfloat16)
    return high, (value - high.astype(jnp.float32)).astype(jnp.bfloat16)


def find(columns, wanted, places, otherwise):
    place = jnp.int32(otherwise)
    for column, here in zip(columns, places):
        place = jnp.where(column == wanted, here, place)
    return place


def left_side(blocks):
    highs, lows = zip(*(split(block.T) for block in blocks))
    return jnp.concatenate(highs + lows + highs, axis=1)


def right_side(columns_of_blocks):
    columns = []
    for blocks in columns_of_blocks:
        highs, lows = zip(*(split(block) for block in blocks))
        columns.append(jnp.concatenate(highs + highs + lows, axis=0))
    return jnp.concatenate(columns, axis=1)


def square_kernel(
    den, cols, out,
    own0, own1, side, za, zb0, zb1, fa, fb, fc,
    c_own, c_side, c_z, c_far, t_own, t_side, t_z, t_far,
    side_s, side_r, far_s, far_r, z_s, z_r,
    mown_s, mown_r, mfar_s, mfar_r, mside_s, mside_r, mz_s, mz_r,
    cs_s, cs_r, cz_s, cz_r, cf_s, cf_r, mc_s, mc_r, local_s, table_s,
):
    blk = lax.axis_index("blk")
    inner = lax.axis_index("inner")
    strips = lax.axis_size("blk")
    parity = lax.rem(blk, 2)
    core = lax.rem(inner, 2)
    chip_x = 2 * (inner // 2) + parity

    def at_x(x):
        x = lax.rem(x, X)
        return (blk - parity + lax.rem(x, 2), 2 * (x // 2) + core)

    right, left = at_x(chip_x + 1), at_x(chip_x + X - 1)
    mirror = (blk, inner + 1 - 2 * core)
    z_to = (lax.rem(blk + strips + 2 - 4 * parity, strips), inner)
    z_from = (lax.rem(blk + strips - 2 + 4 * parity, strips), inner)

    barrier = pltpu.get_barrier_semaphore()
    for device in (right, left, mirror, z_to, z_from):
        pl.semaphore_signal(barrier, inc=1, device_id=device, device_id_type=MESH)

    owned = []
    for row in range(ROWS):
        copy = pltpu.make_async_copy(den.at[row], own0.at[row, pl.ds(0, NZ)], local_s.at[row])
        copy.start()
        owned.append(copy)
    tables = [pltpu.make_async_copy(cols, t_own.at[0], table_s.at[0])]
    tables[0].start()

    none = jnp.zeros(den.shape[2:], jnp.float32)
    for row in range(ROWS):
        own0[row, NZ] = none
        own1[row, NZ] = none
        for half in range(2):
            for buffer in (fa, fb, fc):
                buffer[half, row, PER] = none
            for sd in range(2):
                side[half, sd, row, NZ] = none
                za[half, sd, row, PER] = none
                (zb0, zb1)[row][half, sd, PER] = none

    pl.semaphore_wait(barrier, 5)

    sent = []

    def send(src, dst, s, r, device):
        copy = pltpu.make_async_remote_copy(
            src_ref=src, dst_ref=dst, send_sem=s, recv_sem=r,
            device_id=device, device_id_type=MESH,
        )
        copy.start()
        sent.append(copy)

    def arrived(dst, r):
        pltpu.make_async_remote_copy(
            src_ref=dst, dst_ref=dst, send_sem=r, recv_sem=r,
            device_id=mirror, device_id_type=MESH,
        ).wait_recv()

    def groups(p):
        return (2 * p, 1, 2 - 2 * p)

    def slots(group):
        return pl.ds(PER * group, PER)

    three = pl.ds(0, PER)
    mine = groups(parity)
    theirs = groups(1 - parity)

    for sd, device in ((0, right), (1, left)):
        send(cols, c_side.at[0, sd], cs_s.at[sd], cs_r.at[sd], device)
    for n in range(6):
        g, row = n // 2, n % 2
        cut = slots(mine[g])
        for sd, device in ((0, right), (1, left)):
            send(den.at[row, cut], side.at[0, sd, row, cut],
                 side_s.at[sd, n], side_r.at[sd, n], device)
    send(cols, c_own, mc_s.at[0], mc_r.at[0], mirror)
    for row in range(ROWS):
        send(den.at[row], own1.at[row, pl.ds(0, NZ)], mown_s.at[row], mown_r.at[row], mirror)

    def load_table(k, src, dst):
        copy = pltpu.make_async_copy(src, dst, table_s.at[k])
        copy.start()
        tables.append(copy)

    def z_part(half, m):
        g, row, sd = m // 4, (m // 2) % 2, m % 2
        if g == 0:
            return za.at[half, sd, row, three]
        return (zb0, zb1)[row].at[half, sd, three]

    def z_arrived(m):
        arrived(z_part(0, m), z_r.at[m])
        send(z_part(0, m), z_part(1, m), mz_s.at[m], mz_r.at[m], mirror)

    def far_part(half, row, g):
        return (fa, fb, fc)[g].at[half, row, three]

    def far_arrived(g):
        for row in range(ROWS):
            arrived(far_part(0, row, g), far_r.at[row, g])
            send(far_part(0, row, g), far_part(1, row, g),
                 mfar_s.at[row, g], mfar_r.at[row, g], mirror)

    def side_arrived(n):
        g, row = n // 2, n % 2
        cut = slots(theirs[g])
        for sd in range(2):
            here = side.at[0, sd, row, cut]
            arrived(here, side_r.at[sd, n])
            if g < 2:
                m = 2 * n + sd
                send(here, z_part(0, m), z_s.at[m], z_r.at[m], z_to)
            if row == sd:
                send(here, far_part(0, row, g), far_s.at[row, g], far_r.at[row, g],
                     (right, left)[sd])
            if g > 0:
                m = 4 * (g - 1) + 2 * row + sd
                send(here, side.at[1, sd, row, cut], mside_s.at[m], mside_r.at[m], mirror)

    first = blk * (4 * ROWS) + inner * ROWS

    def wanted(i, group):
        return [t_own[0, i, PER * group + b] for b in range(PER)]

    def add(i, lhs, e, rhs, fresh=False):
        product = jnp.dot(lhs, rhs, preferred_element_type=jnp.float32)
        width = den.shape[3]
        for b in range(PER):
            part = product[:, b * width:(b + 1) * width]
            if fresh:
                out[i, PER * e + b] = part
            else:
                out[i, PER * e + b] += part

    def rights(rows, i, e):
        return right_side([
            [read(find(columns, want, places, empty)) for columns, places, empty, read in rows]
            for want in wanted(i, e)
        ])

    def own_products(buffer, half, fresh):
        def body(i, carry):
            lhs = left_side([
                buffer[row, find([t_own[half, row, PER + a] for a in range(PER)],
                                 first + i, range(PER, 2 * PER), PER)]
                for row in range(ROWS)
            ])
            present = [
                find([t_own[half, row, PER + a] for a in range(PER)], first + i, (1, 1, 1), 0)
                for row in range(ROWS)
            ]
            for e in range(3):
                rows = [
                    ([jnp.where(present[row] == 1, t_own[half, row, PER * e + b], -1)
                      for b in range(PER)],
                     range(PER * e, PER * e + PER), NZ,
                     lambda s, row=row: buffer[row, s])
                    for row in range(ROWS)
                ]
                add(i, lhs, e, rights(rows, i, e), fresh)
            return carry
        lax.fori_loop(0, ROWS, body, 0)

    def general(units, table, row_set, left_group, left_read, parts):
        def body(step, carry):
            unit, i = step // ROWS, lax.rem(step, ROWS)
            lefts, present = [], []
            for row in row_set:
                names = [table(unit, row, PER * left_group + a) for a in range(PER)]
                lefts.append(left_read(unit, row, find(names, first + i, range(PER), 0)))
                present.append(find(names, first + i, (1, 1, 1), 0))
            lhs = left_side(lefts)
            for group, e, read, base, empty in parts:
                rows = [
                    ([jnp.where(present[k] == 1, table(unit, row, PER * group + b), -1)
                      for b in range(PER)],
                     [base + b for b in range(PER)], empty,
                     lambda s, row=row: read(unit, row, s))
                    for k, row in enumerate(row_set)
                ]
                add(i, lhs, e, rights(rows, i, e))
            return carry
        lax.fori_loop(0, units * ROWS, body, 0)

    both = tuple(range(ROWS))

    def side_products():
        name = lambda u, row, s: t_side[u // 2, lax.rem(u, 2), row, s]
        read = lambda u, row, s: side[u // 2, lax.rem(u, 2), row, s]
        low = 2 * parity
        general(4, name, both, low, lambda u, row, a: read(u, row, PER * low + a),
                [(low, 1, read, PER * low, NZ), (1, 2 - 2 * parity, read, PER, NZ)])

    z_name = lambda u, row, s: t_z[u // 2, lax.rem(u, 2), row, s]
    z_left = lambda u, row, a: za[u // 2, lax.rem(u, 2), row, a]

    def za_products():
        general(4, z_name, both, 2 - 2 * parity, z_left,
                [(2 - 2 * parity, 1, z_left, 0, PER)])

    def zb_products(row):
        buffer = (zb0, zb1)[row]
        general(4, z_name, (row,), 2 - 2 * parity, z_left,
                [(1, 2 * parity, lambda u, _, s: buffer[u // 2, lax.rem(u, 2), s], 0, PER)])

    far_name = lambda u, row, s: t_far[u, row, s]
    far_left = lambda u, row, a: fb[u, row, a]

    def far_products(which):
        parts = []
        for g in which:
            buffer = (fa, fb, fc)[g]
            parts.append((mine[g], mine[g], lambda u, row, s, buffer=buffer: buffer[u, row, s],
                          0, PER))
        general(2, far_name, both, 1, far_left, parts)

    for copy in owned:
        copy.wait()
    tables[0].wait()
    own_products(own0, 0, True)

    for sd in range(2):
        arrived(c_side.at[0, sd], cs_r.at[sd])
        send(c_side.at[0, sd], c_z.at[0, sd], cz_s.at[sd], cz_r.at[sd], z_to)
        send(c_side.at[0, sd], c_side.at[1, sd], mc_s.at[1 + sd], mc_r.at[1 + sd], mirror)
    send(c_side.at[0, 0], c_far.at[0], cf_s.at[0], cf_r.at[0], right)
    side_arrived(0)
    arrived(c_own, mc_r.at[0])
    load_table(1, c_own, t_own.at[1])
    for row in range(ROWS):
        arrived(own1.at[row, pl.ds(0, NZ)], mown_r.at[row])
    tables[1].wait()
    own_products(own1, 1, False)
    side_arrived(1)
    arrived(c_far.at[0], cf_r.at[0])
    send(c_far.at[0], c_far.at[1], mc_s.at[3], mc_r.at[3], mirror)
    for sd in range(2):
        arrived(c_z.at[0, sd], cz_r.at[sd])
        send(c_z.at[0, sd], c_z.at[1, sd], mc_s.at[4 + sd], mc_r.at[4 + sd], mirror)
    side_arrived(2)
    z_arrived(0)
    for sd in range(2):
        arrived(c_side.at[1, sd], mc_r.at[1 + sd])
        arrived(c_z.at[1, sd], mc_r.at[4 + sd])
    arrived(c_far.at[1], mc_r.at[3])
    load_table(2, c_side, t_side)
    load_table(3, c_z, t_z)
    load_table(4, c_far, t_far)
    side_arrived(3)
    z_arrived(1)
    side_arrived(4)
    z_arrived(2)
    side_arrived(5)
    z_arrived(3)
    for k in (2, 3, 4):
        tables[k].wait()
    for n in range(2, 6):
        g, row = n // 2, n % 2
        for sd in range(2):
            arrived(side.at[1, sd, row, slots(theirs[g])], mside_r.at[4 * (g - 1) + 2 * row + sd])
    z_arrived(4)
    side_products()
    far_arrived(0)
    z_arrived(5)
    for m in range(4):
        arrived(z_part(1, m), mz_r.at[m])
    za_products()
    z_arrived(6)
    far_arrived(1)
    for m in (4, 5):
        arrived(z_part(1, m), mz_r.at[m])
    zb_products(0)
    for g in (0, 1):
        for row in range(ROWS):
            arrived(far_part(1, row, g), mfar_r.at[row, g])
    far_products((0, 1))
    z_arrived(7)
    far_arrived(2)
    for m in (6, 7):
        arrived(z_part(1, m), mz_r.at[m])
    zb_products(1)
    for row in range(ROWS):
        arrived(far_part(1, row, 2), mfar_r.at[row, 2])
    far_products((2,))
    for copy in sent:
        copy.wait_send()


def square_rows(density, block_cols):
    rows, nz, b, _ = density.shape
    f32, i32 = density.dtype, jnp.int32
    dma = pltpu.SemaphoreType.DMA
    anywhere = pl.BlockSpec(memory_space=pl.ANY)
    vmem, smem = pltpu.VMEM, pltpu.SMEM
    tables = [(rows, nz), (2, 2, rows, nz), (2, 2, rows, nz), (2, rows, nz)]
    return pl.pallas_call(
        square_kernel,
        out_shape=jax.ShapeDtypeStruct(density.shape, f32),
        in_specs=[anywhere, anywhere],
        out_specs=pl.BlockSpec(memory_space=pltpu.VMEM),
        scratch_shapes=[
            vmem((rows, nz + 1, b, b), f32), vmem((rows, nz + 1, b, b), f32),
            vmem((2, 2, rows, nz + 1, b, b), f32),
            vmem((2, 2, rows, PER + 1, b, b), f32),
            vmem((2, 2, PER + 1, b, b), f32), vmem((2, 2, PER + 1, b, b), f32),
            *[vmem((2, rows, PER + 1, b, b), f32)] * 3,
            *[vmem(shape, i32) for shape in tables],
            smem((2, rows, nz), i32), *[smem(shape, i32) for shape in tables[1:]],
            dma((2, 6)), dma((2, 6)), dma((2, 3)), dma((2, 3)), dma((8,)), dma((8,)),
            dma((2,)), dma((2,)), dma((2, 3)), dma((2, 3)),
            dma((8,)), dma((8,)), dma((8,)), dma((8,)),
            dma((2,)), dma((2,)), dma((2,)), dma((2,)), dma((1,)), dma((1,)),
            dma((6,)), dma((6,)), dma((2,)), dma((5,)),
        ],
        compiler_params=pltpu.CompilerParams(
            collective_id=0, has_side_effects=True, vmem_limit_bytes=60 * 2**20),
    )(density, block_cols)


def shards(density, block_cols, targets):
    del targets
    return 2.0 * density - square_rows(density, block_cols)


def solution(mesh):
    return jax.shard_map(
        shards,
        mesh=mesh,
        in_specs=(
            P(("blk", "inner"), None, None, None),
            P(("blk", "inner"), None),
            P(("blk", "inner"), None, None),
        ),
        out_specs=P(("blk", "inner"), None, None, None),
        check_vma=False,
    )
```

time: 322 us -> 67.8 us (0.21)
  waiting for transfers between devices: 209 us -> 0 us
  Pallas kernels: 0 us -> 65.2 us
  other arithmetic: 53 us -> 2.44 us
  local copies, waits for them, and re-layouts: 22.2 us -> 0.01 us
  matrix products: 13.9 us -> 0 us
  between operations: 13.4 us -> 0.02 us
  starting transfers between devices: 10.3 us -> 0 us
    ppermute x2 -> x0, waiting for transfers between devices: 149 us -> none  [shifted(): return lax.ppermute(value, axis, pairs)]
    pallas_call x0 -> x1, Pallas kernels: none -> 65.2 us  [square_rows(): pl.pallas_call(square_kernel, out_shape=jax.ShapeDtypeStruct(density.shap...]
    reduce_scatter x1 -> x0, waiting for transfers between devices: 60.1 us -> none  [shards(): square = lax.psum_scatter(total, 'inner', scatter_dimension=0, tiled=True)]
    scatter-add x3 -> x0, other arithmetic: 39.6 us -> none  [panel_lookup(): panel.at[cells.reshape(-1)]]
    dot_general x3 -> x0, matrix products: 13.9 us -> none  [panel_lookup(): jnp.einsum('kmab,ktac->kmtbc', sources, density, precision=lax.Precision....]
    transpose x3 -> x0, local copies, waits for them, and re-layouts: 13.3 us -> none  [panel_lookup(): jnp.einsum('kmab,ktac->kmtbc', sources, density, precision=lax.Precision....]
    ppermute x2 -> x0, starting transfers between devices: 10.3 us -> none  [shifted(): return lax.ppermute(value, axis, pairs)]
    add x1 -> x0, other arithmetic: 9.34 us -> none  [shards(): total = total.at[:, lower_low:lower_upper_bound].add(from_above)]
  transfers between devices with their start and end apart: 3 -> 0, of which waited for: 3 -> 0; matrix products, arithmetic and copies ran while one was open for 16% -> 0% of each run, Pallas kernels for 0% -> 0%
where the time goes in v3:
time: 67.8 us; the launch traced here: 67.7 us
  Pallas kernels  65.2 us (96%)
  other arithmetic  2.44 us (4%)
    pallas_call x1, Pallas kernels, square_rows(): pl.pallas_call(square_kernel, out_shape=jax.ShapeDtypeStruct(density.shap...  65.2 us
    sub x1, other arithmetic, shards(): return 2.0 * density - square_rows(density, block_cols)  2.44 us

profile of v3, /device:TPU:1, one launch (start us, length us, event | category | flops | bytes accessed | tf_op | source)
XLA Modules:
  0.0 67.7 jit_solution(7215483200257285227)
XLA Ops:
  0.0 0.0 copy-start
  0.0 65.2 %shard_map.28 = f32[2,9,128,128]{3,2,1,0:T(8,128)} custom-call(f32[2,9,128,128]{3,2,1,0:T(8,128)} %den.1, s32[2,9]{1,0:T(2,128)} %cols.1), custom_call_target="tpu_custom_call" | custom-call | tf_op jit(solution)/shard_map/pallas_call | solution.py:344
  65.2 0.0 copy-done
  65.3 2.4 %multiply_subtract_fusion = f32[2,9,128,128]{3,2,1,0:T(8,128)} fusion(f32[2,9,128,128]{3,2,1,0:T(8,128)} %shard_map.28, f32[2,9,128,128]{3,2,1,0:T(8,128)S(1)} %copy-done), kind=kLoop, calls=%fused_computation | loop fusion | flops 589824 | bytes 3538944 | tf_op jit(solution)/shard_map/sub | solution.py:370
Async XLA Ops:
  0.0 65.3 %copy-start = (f32[2,9,128,128]{3,2,1,0:T(8,128)S(1)}, f32[2,9,128,128]{3,2,1,0:T(8,128)}, u32[]{:S(2)}) copy-start(f32[2,9,128,128]{3,2,1,0:T(8,128)} %den.1) | copy-start | bytes 3538948

commit v4 on v3

--- a/solution.py
+++ b/solution.py
@@ -10,6 +10,7 @@
 NZ = 9
 X = 4
 ROWS = 2
+SIDE = ((0, 0, 0, 1), (0, 0, 1, 2), (1, 0, 0, 3), (0, 1, 0, 3), (1, 1, 0, 3), (0, 2, 0, 3), (1, 2, 0, 3))
 
 
 def split(value):
@@ -40,7 +41,7 @@
 def square_kernel(
     den, cols, out,
     own0, own1, side, za, zb0, zb1, fa, fb, fc,
-    c_own, c_side, c_z, c_far, t_own, t_side, t_z, t_far,
+    lz, lf, c_own, c_side, c_z, c_far, t_own, t_side, t_z, t_far,
     side_s, side_r, far_s, far_r, z_s, z_r,
     mown_s, mown_r, mfar_s, mfar_r, mside_s, mside_r, mz_s, mz_r,
     cs_s, cs_r, cz_s, cz_r, cf_s, cf_r, mc_s, mc_r, local_s, table_s,
@@ -57,12 +58,13 @@
         return (blk - parity + lax.rem(x, 2), 2 * (x // 2) + core)
 
     right, left = at_x(chip_x + 1), at_x(chip_x + X - 1)
+    far = at_x(chip_x + 2)
     mirror = (blk, inner + 1 - 2 * core)
     z_to = (lax.rem(blk + strips + 2 - 4 * parity, strips), inner)
     z_from = (lax.rem(blk + strips - 2 + 4 * parity, strips), inner)
 
     barrier = pltpu.get_barrier_semaphore()
-    for device in (right, left, mirror, z_to, z_from):
+    for device in (right, left, far, mirror, z_to, z_from):
         pl.semaphore_signal(barrier, inc=1, device_id=device, device_id_type=MESH)
 
     owned = []
@@ -85,7 +87,7 @@
                 za[half, sd, row, PER] = none
                 (zb0, zb1)[row][half, sd, PER] = none
 
-    pl.semaphore_wait(barrier, 5)
+    pl.semaphore_wait(barrier, 6)
 
     sent = []
 
@@ -106,8 +108,8 @@
     def groups(p):
         return (2 * p, 1, 2 - 2 * p)
 
-    def slots(group):
-        return pl.ds(PER * group, PER)
+    def slots(group, first=0, count=PER):
+        return pl.ds(PER * group + first, count)
 
     three = pl.ds(0, PER)
     mine = groups(parity)
@@ -115,9 +117,9 @@
 
     for sd, device in ((0, right), (1, left)):
         send(cols, c_side.at[0, sd], cs_s.at[sd], cs_r.at[sd], device)
-    for n in range(6):
-        g, row = n // 2, n % 2
-        cut = slots(mine[g])
+    send(cols, c_far.at[0], cf_s.at[0], cf_r.at[0], far)
+    for n, (row, g, low, count) in enumerate(SIDE):
+        cut = slots(mine[g], low, count)
         for sd, device in ((0, right), (1, left)):
             send(den.at[row, cut], side.at[0, sd, row, cut],
                  side_s.at[sd, n], side_r.at[sd, n], device)
@@ -130,40 +132,73 @@
         copy.start()
         tables.append(copy)
 
-    def z_part(half, m):
-        g, row, sd = m // 4, (m // 2) % 2, m % 2
-        if g == 0:
-            return za.at[half, sd, row, three]
-        return (zb0, zb1)[row].at[half, sd, three]
+    def z_part(half, sd, piece):
+        row, g, low, count = piece
+        cut = pl.ds(low, count)
+        return za.at[half, sd, row, cut] if g == 0 else (zb0, zb1)[row].at[half, sd, cut]
+
+    z_pieces = [(n, sd) for n, piece in enumerate(SIDE) if piece[1] < 2 for sd in range(2)]
 
     def z_arrived(m):
-        arrived(z_part(0, m), z_r.at[m])
-        send(z_part(0, m), z_part(1, m), mz_s.at[m], mz_r.at[m], mirror)
-
-    def far_part(half, row, g):
-        return (fa, fb, fc)[g].at[half, row, three]
-
-    def far_arrived(g):
+        n, sd = z_pieces[m]
+        piece = SIDE[n]
+        arrived(z_part(0, sd, piece), z_r.at[m])
+        send(z_part(0, sd, piece), z_part(1, sd, piece), mz_s.at[m], mz_r.at[m], mirror)
+
+    def z_mirrored(m):
+        n, sd = z_pieces[m]
+        arrived(z_part(1, sd, SIDE[n]), mz_r.at[m])
+
+    def far_part(half, piece):
+        row, g, low, count = piece
+        return (fa, fb, fc)[g].at[half, row, pl.ds(low, count)]
+
+    def far_pieces(piece):
+        row, g, low, count = piece
+        return [piece] if g < 2 else [(row, g, 0, 2), (row, g, 2, 1)]
+
+    far_list = [(row, k, piece) for row in range(ROWS) for k, piece in
+                enumerate(p for q in SIDE if q[0] == row for p in far_pieces(q))]
+
+    def far_wait(half, g, sems, row, last=None):
+        for r, k, piece in far_list:
+            if r == row and piece[1] == g and (last is None or last == (piece[2] == 2)):
+                arrived(far_part(half, piece), sems.at[r, k])
+                if half == 0:
+                    send(far_part(0, piece), far_part(1, piece),
+                         mfar_s.at[r, k], mfar_r.at[r, k], mirror)
+
+    def far_arrived(g, last=None):
         for row in range(ROWS):
-            arrived(far_part(0, row, g), far_r.at[row, g])
-            send(far_part(0, row, g), far_part(1, row, g),
-                 mfar_s.at[row, g], mfar_r.at[row, g], mirror)
+            far_wait(0, g, far_r, row, last)
+
+    def far_mirrored(g):
+        for row in range(ROWS):
+            far_wait(1, g, mfar_r, row)
 
     def side_arrived(n):
-        g, row = n // 2, n % 2
-        cut = slots(theirs[g])
+        row, g, low, count = SIDE[n]
         for sd in range(2):
-            here = side.at[0, sd, row, cut]
+            here = side.at[0, sd, row, slots(theirs[g], low, count)]
             arrived(here, side_r.at[sd, n])
             if g < 2:
                 m = 2 * n + sd
-                send(here, z_part(0, m), z_s.at[m], z_r.at[m], z_to)
+                send(here, z_part(0, sd, SIDE[n]), z_s.at[m], z_r.at[m], z_to)
             if row == sd:
-                send(here, far_part(0, row, g), far_s.at[row, g], far_r.at[row, g],
-                     (right, left)[sd])
+                for r, k, piece in far_list:
+                    if r == row and piece in far_pieces(SIDE[n]):
+                        there = side.at[0, sd, row, slots(theirs[g], piece[2], piece[3])]
+                        send(there, far_part(0, piece), far_s.at[row, k], far_r.at[row, k],
+                             (right, left)[sd])
             if g > 0:
-                m = 4 * (g - 1) + 2 * row + sd
-                send(here, side.at[1, sd, row, cut], mside_s.at[m], mside_r.at[m], mirror)
+                send(here, side.at[1, sd, row, slots(theirs[g], low, count)],
+                     mside_s.at[sd, n], mside_r.at[sd, n], mirror)
+
+    def side_mirrored():
+        for n, (row, g, low, count) in enumerate(SIDE):
+            if g > 0:
+                for sd in range(2):
+                    arrived(side.at[1, sd, row, slots(theirs[g], low, count)], mside_r.at[sd, n])
 
     first = blk * (4 * ROWS) + inner * ROWS
 
@@ -209,58 +244,72 @@
             return carry
         lax.fori_loop(0, ROWS, body, 0)
 
-    def general(units, table, row_set, left_group, left_read, parts):
-        def body(step, carry):
-            unit, i = step // ROWS, lax.rem(step, ROWS)
-            lefts, present = [], []
-            for row in row_set:
-                names = [table(unit, row, PER * left_group + a) for a in range(PER)]
-                lefts.append(left_read(unit, row, find(names, first + i, range(PER), 0)))
-                present.append(find(names, first + i, (1, 1, 1), 0))
-            lhs = left_side(lefts)
-            for group, e, read, base, empty in parts:
-                rows = [
-                    ([jnp.where(present[k] == 1, table(unit, row, PER * group + b), -1)
-                      for b in range(PER)],
-                     [base + b for b in range(PER)], empty,
-                     lambda s, row=row: read(unit, row, s))
-                    for k, row in enumerate(row_set)
-                ]
+    def lefts(names, reads, i):
+        return left_side([read(find(name, first + i, range(PER), 0))
+                          for name, read in zip(names, reads)])
+
+    def guarded(name, columns, i):
+        present = find(name, first + i, (1, 1, 1), 0) == 1
+        return [jnp.where(present, column, -1) for column in columns]
+
+    def entries(table, index, group):
+        return [table[(*index, PER * group + b)] for b in range(PER)]
+
+    two = [(half, sd) for half in range(2) for sd in range(2)]
+    pair = [(half, row) for half in range(2) for row in range(ROWS)]
+
+    def side_products(i):
+        low = 2 * parity
+        for row in range(ROWS):
+            names = [entries(t_side, (h, sd, row), low) for h, sd in two]
+            reads = [lambda s, h=h, sd=sd: side[h, sd, row, s] for h, sd in two]
+            lhs = lefts(names, [lambda a, r=r: r(PER * low + a) for r in reads], i)
+            for group, e in ((low, 1), (1, 2 - 2 * parity)):
+                rows = [(guarded(name, entries(t_side, (h, sd, row), group), i),
+                         [PER * group + b for b in range(PER)], NZ, read)
+                        for name, (h, sd), read in zip(names, two, reads)]
                 add(i, lhs, e, rights(rows, i, e))
+
+    z_group = 2 - 2 * parity
+
+    def z_lefts(i):
+        for row in range(ROWS):
+            names = [entries(t_z, (h, sd, row), z_group) for h, sd in two]
+            reads = [lambda s, h=h, sd=sd: za[h, sd, row, s] for h, sd in two]
+            lz[row, i] = lefts(names, reads, i)
+
+    def z_products(row, group, e, read, i):
+        rows = [(guarded(entries(t_z, (h, sd, row), z_group), entries(t_z, (h, sd, row), group), i),
+                 range(PER), PER, lambda s, h=h, sd=sd: read(h, sd, s))
+                for h, sd in two]
+        add(i, lz[row, i], e, rights(rows, i, e))
+
+    def za_products(i):
+        for row in range(ROWS):
+            z_products(row, z_group, 1, lambda h, sd, s: za[h, sd, row, s], i)
+
+    def zb_products(row, i):
+        buffer = (zb0, zb1)[row]
+        z_products(row, 1, 2 * parity, lambda h, sd, s: buffer[h, sd, s], i)
+
+    def far_lefts(i):
+        names = [entries(t_far, (h, row), 1) for h, row in pair]
+        reads = [lambda s, h=h, row=row: fb[h, row, s] for h, row in pair]
+        lf[i] = lefts(names, reads, i)
+
+    def far_products(g, i):
+        buffer, group = (fa, fb, fc)[g], mine[g]
+        rows = [(guarded(entries(t_far, (h, row), 1), entries(t_far, (h, row), group), i),
+                 range(PER), PER, lambda s, h=h, row=row: buffer[h, row, s])
+                for h, row in pair]
+        add(i, lf[i], group, rights(rows, i, group))
+
+    def each_row(*steps):
+        def body(i, carry):
+            for step in steps:
+                step(i)
             return carry
-        lax.fori_loop(0, units * ROWS, body, 0)
-
-    both = tuple(range(ROWS))
-
-    def side_products():
-        name = lambda u, row, s: t_side[u // 2, lax.rem(u, 2), row, s]
-        read = lambda u, row, s: side[u // 2, lax.rem(u, 2), row, s]
-        low = 2 * parity
-        general(4, name, both, low, lambda u, row, a: read(u, row, PER * low + a),
-                [(low, 1, read, PER * low, NZ), (1, 2 - 2 * parity, read, PER, NZ)])
-
-    z_name = lambda u, row, s: t_z[u // 2, lax.rem(u, 2), row, s]
-    z_left = lambda u, row, a: za[u // 2, lax.rem(u, 2), row, a]
-
-    def za_products():
-        general(4, z_name, both, 2 - 2 * parity, z_left,
-                [(2 - 2 * parity, 1, z_left, 0, PER)])
-
-    def zb_products(row):
-        buffer = (zb0, zb1)[row]
-        general(4, z_name, (row,), 2 - 2 * parity, z_left,
-                [(1, 2 * parity, lambda u, _, s: buffer[u // 2, lax.rem(u, 2), s], 0, PER)])
-
-    far_name = lambda u, row, s: t_far[u, row, s]
-    far_left = lambda u, row, a: fb[u, row, a]
-
-    def far_products(which):
-        parts = []
-        for g in which:
-            buffer = (fa, fb, fc)[g]
-            parts.append((mine[g], mine[g], lambda u, row, s, buffer=buffer: buffer[u, row, s],
-                          0, PER))
-        general(2, far_name, both, 1, far_left, parts)
+        lax.fori_loop(0, ROWS, body, 0)
 
     for copy in owned:
         copy.wait()
@@ -271,22 +320,23 @@
         arrived(c_side.at[0, sd], cs_r.at[sd])
         send(c_side.at[0, sd], c_z.at[0, sd], cz_s.at[sd], cz_r.at[sd], z_to)
         send(c_side.at[0, sd], c_side.at[1, sd], mc_s.at[1 + sd], mc_r.at[1 + sd], mirror)
-    send(c_side.at[0, 0], c_far.at[0], cf_s.at[0], cf_r.at[0], right)
     side_arrived(0)
+    side_arrived(1)
     arrived(c_own, mc_r.at[0])
     load_table(1, c_own, t_own.at[1])
     for row in range(ROWS):
         arrived(own1.at[row, pl.ds(0, NZ)], mown_r.at[row])
     tables[1].wait()
     own_products(own1, 1, False)
-    side_arrived(1)
+    side_arrived(2)
     arrived(c_far.at[0], cf_r.at[0])
     send(c_far.at[0], c_far.at[1], mc_s.at[3], mc_r.at[3], mirror)
     for sd in range(2):
         arrived(c_z.at[0, sd], cz_r.at[sd])
         send(c_z.at[0, sd], c_z.at[1, sd], mc_s.at[4 + sd], mc_r.at[4 + sd], mirror)
-    side_arrived(2)
+    side_arrived(3)
     z_arrived(0)
+    z_arrived(1)
     for sd in range(2):
         arrived(c_side.at[1, sd], mc_r.at[1 + sd])
         arrived(c_z.at[1, sd], mc_r.at[4 + sd])
@@ -294,42 +344,41 @@
     load_table(2, c_side, t_side)
     load_table(3, c_z, t_z)
     load_table(4, c_far, t_far)
-    side_arrived(3)
-    z_arrived(1)
     side_arrived(4)
     z_arrived(2)
+    z_arrived(3)
     side_arrived(5)
-    z_arrived(3)
+    z_arrived(4)
+    side_arrived(6)
+    z_arrived(5)
     for k in (2, 3, 4):
         tables[k].wait()
-    for n in range(2, 6):
-        g, row = n // 2, n % 2
-        for sd in range(2):
-            arrived(side.at[1, sd, row, slots(theirs[g])], mside_r.at[4 * (g - 1) + 2 * row + sd])
-    z_arrived(4)
-    side_products()
+    side_mirrored()
+    each_row(side_products)
+    z_arrived(6)
     far_arrived(0)
-    z_arrived(5)
-    for m in range(4):
-        arrived(z_part(1, m), mz_r.at[m])
-    za_products()
-    z_arrived(6)
+    z_arrived(7)
+    for m in range(6):
+        z_mirrored(m)
+    each_row(z_lefts, za_products)
+    z_arrived(8)
     far_arrived(1)
-    for m in (4, 5):
-        arrived(z_part(1, m), mz_r.at[m])
-    zb_products(0)
+    for m in (6, 7):
+        z_mirrored(m)
+    each_row(lambda i: zb_products(0, i))
     for g in (0, 1):
-        for row in range(ROWS):
-            arrived(far_part(1, row, g), mfar_r.at[row, g])
-    far_products((0, 1))
-    z_arrived(7)
-    far_arrived(2)
-    for m in (6, 7):
-        arrived(z_part(1, m), mz_r.at[m])
-    zb_products(1)
-    for row in range(ROWS):
-        arrived(far_part(1, row, 2), mfar_r.at[row, 2])
-    far_products((2,))
+        far_mirrored(g)
+    each_row(far_lefts, lambda i: far_products(0, i), lambda i: far_products(1, i))
+    z_arrived(9)
+    far_arrived(2, False)
+    for m in (8, 9):
+        z_mirrored(m)
+    for i in range(ROWS):
+        zb_products(1, i)
+    far_arrived(2, True)
+    far_mirrored(2)
+    for i in range(ROWS):
+        far_products(2, i)
     for copy in sent:
         copy.wait_send()
 
@@ -352,11 +401,12 @@
             vmem((2, 2, rows, PER + 1, b, b), f32),
             vmem((2, 2, PER + 1, b, b), f32), vmem((2, 2, PER + 1, b, b), f32),
             *[vmem((2, rows, PER + 1, b, b), f32)] * 3,
+            vmem((rows, rows, b, 12 * b), jnp.bfloat16), vmem((rows, b, 12 * b), jnp.bfloat16),
             *[vmem(shape, i32) for shape in tables],
             smem((2, rows, nz), i32), *[smem(shape, i32) for shape in tables[1:]],
-            dma((2, 6)), dma((2, 6)), dma((2, 3)), dma((2, 3)), dma((8,)), dma((8,)),
-            dma((2,)), dma((2,)), dma((2, 3)), dma((2, 3)),
-            dma((8,)), dma((8,)), dma((8,)), dma((8,)),
+            dma((2, 7)), dma((2, 7)), dma((2, 5)), dma((2, 5)), dma((10,)), dma((10,)),
+            dma((2,)), dma((2,)), dma((2, 5)), dma((2, 5)),
+            dma((2, 7)), dma((2, 7)), dma((10,)), dma((10,)),
             dma((2,)), dma((2,)), dma((2,)), dma((2,)), dma((1,)), dma((1,)),
             dma((6,)), dma((6,)), dma((2,)), dma((5,)),
         ],

time: 67.8 us -> 59.7 us (0.88)
  Pallas kernels: 65.2 us -> 57.1 us
    pallas_call x1, Pallas kernels: 65.2 us -> 57.1 us  [square_rows(): pl.pallas_call(square_kernel, out_shape=jax.ShapeDtypeStruct(density.shap...]
where the time goes in v4:
time: 59.7 us; the launch traced here: 59.6 us
  Pallas kernels  57.1 us (96%)
  other arithmetic  2.44 us (4%)
    pallas_call x1, Pallas kernels, square_rows(): pl.pallas_call(square_kernel, out_shape=jax.ShapeDtypeStruct(density.shap...  57.1 us
    sub x1, other arithmetic, shards(): return 2.0 * density - square_rows(density, block_cols)  2.44 us

profile of v4, /device:TPU:1, one launch (start us, length us, event | category | flops | bytes accessed | tf_op | source)
XLA Modules:
  0.0 59.6 jit_solution(58786552597974266)
XLA Ops:
  0.0 0.0 copy-start
  0.0 57.1 %shard_map.28 = f32[2,9,128,128]{3,2,1,0:T(8,128)} custom-call(f32[2,9,128,128]{3,2,1,0:T(8,128)} %den.1, s32[2,9]{1,0:T(2,128)} %cols.1), custom_call_target="tpu_custom_call" | custom-call | tf_op jit(solution)/shard_map/pallas_call | solution.py:393
  57.1 0.0 copy-done
  57.1 2.4 %multiply_subtract_fusion = f32[2,9,128,128]{3,2,1,0:T(8,128)} fusion(f32[2,9,128,128]{3,2,1,0:T(8,128)} %shard_map.28, f32[2,9,128,128]{3,2,1,0:T(8,128)S(1)} %copy-done), kind=kLoop, calls=%fused_computation | loop fusion | flops 589824 | bytes 3538944 | tf_op jit(solution)/shard_map/sub | solution.py:420
Async XLA Ops:
  0.0 57.1 %copy-start = (f32[2,9,128,128]{3,2,1,0:T(8,128)S(1)}, f32[2,9,128,128]{3,2,1,0:T(8,128)}, u32[]{:S(2)}) copy-start(f32[2,9,128,128]{3,2,1,0:T(8,128)} %den.1) | copy-start | bytes 3538948

commit v5 on v4

v5 whole, which is shorter than its diff:
```python
import jax
import jax.numpy as jnp
from jax import lax
from jax.experimental import pallas as pl
from jax.experimental.pallas import tpu as pltpu
from jax.sharding import PartitionSpec as P

MESH = pl.DeviceIdType.MESH
PER = 3
NZ = 9
X = 4
ROWS = 2
SIDE = ((0, 0, 0, 1), (0, 0, 1, 2), (1, 0, 0, 3), (0, 1, 0, 3), (1, 1, 0, 3), (0, 2, 0, 3), (1, 2, 0, 3))


def split(value):
    high = value.astype(jnp.bfloat16)
    return high, (value - high.astype(jnp.float32)).astype(jnp.bfloat16)


def find(columns, wanted, places, otherwise):
    place = jnp.int32(otherwise)
    for column, here in zip(columns, places):
        place = jnp.where(column == wanted, here, place)
    return place


def left_side(blocks):
    highs, lows = zip(*(split(block.T) for block in blocks))
    return jnp.concatenate(highs + lows + highs, axis=1)


def right_side(columns_of_blocks):
    columns = []
    for blocks in columns_of_blocks:
        highs, lows = zip(*(split(block) for block in blocks))
        columns.append(jnp.concatenate(highs + highs + lows, axis=0))
    return jnp.concatenate(columns, axis=1)


def square_kernel(
    den, cols, out,
    own0, own1, side0, side1, side2, za, fa, fb, x_out, x_in, z_out, z_in,
    lf, c_own, c_side, c_z, c_far, c_next, t_own, t_side, t_z, t_far, t_next,
    side_s, side_r, far_s, far_r, z_s, z_r,
    mown_s, mown_r, mfar_s, mfar_r, mside_s, mside_r, mz_s, mz_r,
    cs_s, cs_r, cz_s, cz_r, cf_s, cf_r, cn_s, cn_r, mc_s, mc_r,
    xp_s, xp_r, zp_s, zp_r, local_s, table_s,
):
    blk = lax.axis_index("blk")
    inner = lax.axis_index("inner")
    strips = lax.axis_size("blk")
    parity = lax.rem(blk, 2)
    core = lax.rem(inner, 2)
    chip_x = 2 * (inner // 2) + parity

    def at_x(x):
        x = lax.rem(x, X)
        return (blk - parity + lax.rem(x, 2), 2 * (x // 2) + core)

    right, left = at_x(chip_x + 1), at_x(chip_x + X - 1)
    far = at_x(chip_x + 2)
    mirror = (blk, inner + 1 - 2 * core)
    z_to = (lax.rem(blk + strips + 2 - 4 * parity, strips), inner)
    z_from = (lax.rem(blk + strips - 2 + 4 * parity, strips), inner)

    barrier = pltpu.get_barrier_semaphore()
    for device in (right, left, far, mirror, z_to, z_from):
        pl.semaphore_signal(barrier, inc=1, device_id=device, device_id_type=MESH)

    owned = []
    for row in range(ROWS):
        copy = pltpu.make_async_copy(den.at[row], own0.at[row, pl.ds(0, NZ)], local_s.at[row])
        copy.start()
        owned.append(copy)
    tables = [pltpu.make_async_copy(cols, t_own.at[0], table_s.at[0])]
    tables[0].start()

    none = jnp.zeros(den.shape[2:], jnp.float32)
    for row in range(ROWS):
        own0[row, NZ] = none
        own1[row, NZ] = none
        for half in range(2):
            for buffer in (fa, fb):
                buffer[half, row, PER] = none
            for sd in range(2):
                for buffer in (side0, side1, side2):
                    buffer[half, sd, row, PER] = none
                za[half, sd, row, PER] = none

    pl.semaphore_wait(barrier, 6)

    sent = []

    def send(src, dst, s, r, device):
        copy = pltpu.make_async_remote_copy(
            src_ref=src, dst_ref=dst, send_sem=s, recv_sem=r,
            device_id=device, device_id_type=MESH,
        )
        copy.start()
        sent.append(copy)

    def arrived(dst, r):
        pltpu.make_async_remote_copy(
            src_ref=dst, dst_ref=dst, send_sem=r, recv_sem=r,
            device_id=mirror, device_id_type=MESH,
        ).wait_recv()

    def groups(p):
        return (2 * p, 1, 2 - 2 * p)

    def slots(group, first=0, count=PER):
        return pl.ds(PER * group + first, count)

    three = pl.ds(0, PER)
    mine = groups(parity)
    theirs = groups(1 - parity)

    def side_part(half, sd, piece):
        row, g, low, count = piece
        return (side0, side1, side2)[g].at[half, sd, row, pl.ds(low, count)]

    for sd, device in ((0, right), (1, left)):
        send(cols, c_side.at[0, sd], cs_s.at[sd], cs_r.at[sd], device)
    send(cols, c_far.at[0], cf_s.at[0], cf_r.at[0], far)
    send(cols, c_next, cn_s.at[0], cn_r.at[0], z_from)
    for n, (row, g, low, count) in enumerate(SIDE):
        cut = slots(mine[g], low, count)
        for sd, device in ((0, right), (1, left)):
            send(den.at[row, cut], side_part(0, sd, SIDE[n]),
                 side_s.at[sd, n], side_r.at[sd, n], device)
    send(cols, c_own, mc_s.at[0], mc_r.at[0], mirror)
    for row in range(ROWS):
        send(den.at[row], own1.at[row, pl.ds(0, NZ)], mown_s.at[row], mown_r.at[row], mirror)

    def load_table(k, src, dst):
        copy = pltpu.make_async_copy(src, dst, table_s.at[k])
        copy.start()
        tables.append(copy)

    def z_part(half, sd, piece):
        row, g, low, count = piece
        return za.at[half, sd, row, pl.ds(low, count)]

    z_pieces = [(n, sd) for n, piece in enumerate(SIDE) if piece[1] == 0 for sd in range(2)]

    def z_arrived(m):
        n, sd = z_pieces[m]
        piece = SIDE[n]
        arrived(z_part(0, sd, piece), z_r.at[m])
        send(z_part(0, sd, piece), z_part(1, sd, piece), mz_s.at[m], mz_r.at[m], mirror)

    def z_mirrored(m):
        n, sd = z_pieces[m]
        arrived(z_part(1, sd, SIDE[n]), mz_r.at[m])

    def far_part(half, piece):
        row, g, low, count = piece
        return (fa, fb)[g].at[half, row, pl.ds(low, count)]

    far_list = [(row, k, piece) for row in range(ROWS) for k, piece in
                enumerate(p for p in SIDE if p[0] == row and p[1] < 2)]

    def far_arrived(g):
        for row, k, piece in far_list:
            if piece[1] == g:
                arrived(far_part(0, piece), far_r.at[row, k])
                send(far_part(0, piece), far_part(1, piece),
                     mfar_s.at[row, k], mfar_r.at[row, k], mirror)

    def far_mirrored(g):
        for row, k, piece in far_list:
            if piece[1] == g:
                arrived(far_part(1, piece), mfar_r.at[row, k])

    def side_arrived(n):
        row, g, low, count = SIDE[n]
        for sd in range(2):
            here = side_part(0, sd, SIDE[n])
            arrived(here, side_r.at[sd, n])
            if g == 0:
                m = 2 * n + sd
                send(here, z_part(0, sd, SIDE[n]), z_s.at[m], z_r.at[m], z_to)
            for r, k, piece in far_list:
                if row == sd and piece == SIDE[n]:
                    send(here, far_part(0, piece), far_s.at[row, k], far_r.at[row, k],
                         (right, left)[sd])
            send(here, side_part(1, sd, SIDE[n]), mside_s.at[sd, n], mside_r.at[sd, n], mirror)

    def side_mirrored(which):
        for n in which:
            for sd in range(2):
                arrived(side_part(1, sd, SIDE[n]), mside_r.at[sd, n])

    first = blk * (4 * ROWS) + inner * ROWS

    def wanted(i, group):
        return [t_own[0, i, PER * group + b] for b in range(PER)]

    def parts(lhs, rhs):
        product = jnp.dot(lhs, rhs, preferred_element_type=jnp.float32)
        width = den.shape[3]
        return [product[:, b * width:(b + 1) * width] for b in range(PER)]

    def add(i, e, blocks, fresh=False):
        for b, block in enumerate(blocks):
            if fresh:
                out[i, PER * e + b] = block
            else:
                out[i, PER * e + b] += block

    def rights(rows, want):
        return right_side([
            [read(find(columns, column, places, empty)) for columns, places, empty, read in rows]
            for column in want
        ])

    def own_products(buffer, half, fresh):
        def body(i, carry):
            lhs = left_side([
                buffer[row, find([t_own[half, row, PER + a] for a in range(PER)],
                                 first + i, range(PER, 2 * PER), PER)]
                for row in range(ROWS)
            ])
            present = [
                find([t_own[half, row, PER + a] for a in range(PER)], first + i, (1, 1, 1), 0)
                for row in range(ROWS)
            ]
            for e in range(3):
                rows = [
                    ([jnp.where(present[row] == 1, t_own[half, row, PER * e + b], -1)
                      for b in range(PER)],
                     range(PER * e, PER * e + PER), NZ,
                     lambda s, row=row: buffer[row, s])
                    for row in range(ROWS)
                ]
                add(i, e, parts(lhs, rights(rows, wanted(i, e))), fresh)
            return carry
        lax.fori_loop(0, ROWS, body, 0)

    def lefts(names, reads, target):
        return left_side([read(find(name, target, range(PER), 0))
                          for name, read in zip(names, reads)])

    def guarded(name, columns, target):
        present = find(name, target, (1, 1, 1), 0) == 1
        return [jnp.where(present, column, -1) for column in columns]

    def entries(table, index, group):
        return [table[(*index, PER * group + b)] for b in range(PER)]

    two = [(half, sd) for half in range(2) for sd in range(2)]
    pair = [(half, row) for half in range(2) for row in range(ROWS)]

    def from_side(where, left_place, target, parts_wanted):
        buffers = (side0, side1, side2)
        names = [entries(t_side, index, theirs[left_place]) for index in where]

        def reader(place, index):
            return lambda s: buffers[place][(*index, s)]

        lhs = lefts(names, [reader(left_place, index) for index in where], target)
        for place, want in parts_wanted:
            rows = [(guarded(name, entries(t_side, index, theirs[place]), target),
                     range(PER), PER, reader(place, index))
                    for name, index in zip(names, where)]
            yield parts(lhs, rights(rows, want))

    def side_products(i):
        places = ((2, 1), (1, 2 - 2 * parity))
        for row in range(ROWS):
            blocks = from_side([(h, sd, row) for h, sd in two], 2, first + i,
                               [(place, wanted(i, e)) for place, e in places])
            for (_, e), block in zip(places, blocks):
                add(i, e, block)

    def first_of(device):
        return device[0] * (4 * ROWS) + device[1] * ROWS

    def x_partial(direction):
        device = (right, left)[direction]
        want = entries(t_side, (0, 1 - direction, direction), theirs[2])
        where = [(h, direction, row) for h, row in pair]
        (blocks,) = from_side(where, 1, first_of(device) + direction, [(2, want)])
        for b, block in enumerate(blocks):
            x_out[direction, b] = block

    def z_partial(i):
        want = [t_next[i, PER * 2 * parity + b] for b in range(PER)]
        sums = None
        for row in range(ROWS):
            (blocks,) = from_side([(h, sd, row) for h, sd in two], 0,
                                  first_of(z_to) + i, [(1, want)])
            sums = blocks if sums is None else [a + b for a, b in zip(sums, blocks)]
        for b, block in enumerate(sums):
            z_out[i, b] = block

    z_group = 2 - 2 * parity

    def za_products(i):
        for row in range(ROWS):
            names = [entries(t_z, (h, sd, row), z_group) for h, sd in two]
            reads = [lambda s, h=h, sd=sd: za[h, sd, row, s] for h, sd in two]
            rows = [(guarded(name, name, first + i), range(PER), PER, read)
                    for name, read in zip(names, reads)]
            add(i, 1, parts(lefts(names, reads, first + i), rights(rows, wanted(i, 1))))

    def far_lefts(i):
        names = [entries(t_far, (h, row), 1) for h, row in pair]
        reads = [lambda s, h=h, row=row: fb[h, row, s] for h, row in pair]
        lf[i] = lefts(names, reads, first + i)

    def far_products(g, i):
        buffer, group = (fa, fb)[g], mine[g]
        rows = [(guarded(entries(t_far, (h, row), 1), entries(t_far, (h, row), group), first + i),
                 range(PER), PER, lambda s, h=h, row=row: buffer[h, row, s])
                for h, row in pair]
        add(i, group, parts(lf[i], rights(rows, wanted(i, group))))

    def each_row(*steps):
        def body(i, carry):
            for step in steps:
                step(i)
            return carry
        lax.fori_loop(0, ROWS, body, 0)

    for copy in owned:
        copy.wait()
    tables[0].wait()
    own_products(own0, 0, True)

    for sd in range(2):
        arrived(c_side.at[0, sd], cs_r.at[sd])
        send(c_side.at[0, sd], c_z.at[0, sd], cz_s.at[sd], cz_r.at[sd], z_to)
        send(c_side.at[0, sd], c_side.at[1, sd], mc_s.at[1 + sd], mc_r.at[1 + sd], mirror)
    side_arrived(0)
    side_arrived(1)
    arrived(c_own, mc_r.at[0])
    load_table(1, c_own, t_own.at[1])
    for row in range(ROWS):
        arrived(own1.at[row, pl.ds(0, NZ)], mown_r.at[row])
    tables[1].wait()
    own_products(own1, 1, False)
    side_arrived(2)
    arrived(c_far.at[0], cf_r.at[0])
    send(c_far.at[0], c_far.at[1], mc_s.at[3], mc_r.at[3], mirror)
    for sd in range(2):
        arrived(c_z.at[0, sd], cz_r.at[sd])
        send(c_z.at[0, sd], c_z.at[1, sd], mc_s.at[4 + sd], mc_r.at[4 + sd], mirror)
    arrived(c_next, cn_r.at[0])
    z_arrived(0)
    z_arrived(1)
    for sd in range(2):
        arrived(c_side.at[1, sd], mc_r.at[1 + sd])
        arrived(c_z.at[1, sd], mc_r.at[4 + sd])
    arrived(c_far.at[1], mc_r.at[3])
    load_table(2, c_side, t_side)
    load_table(3, c_z, t_z)
    load_table(4, c_far, t_far)
    load_table(5, c_next, t_next)
    side_arrived(3)
    z_arrived(2)
    z_arrived(3)
    side_arrived(4)
    for k in (2, 3, 4, 5):
        tables[k].wait()
    side_mirrored(range(5))
    each_row(z_partial)
    z_arrived(4)
    z_arrived(5)
    for i in range(ROWS):
        send(z_out.at[i], z_in.at[i], zp_s.at[i], zp_r.at[i], z_to)
    side_arrived(5)
    for m in range(6):
        z_mirrored(m)
    each_row(za_products)
    side_arrived(6)
    side_mirrored((5, 6))
    for direction in range(2):
        x_partial(direction)
    far_arrived(0)
    for direction, device in enumerate((right, left)):
        send(x_out.at[direction], x_in.at[direction],
             xp_s.at[direction], xp_r.at[direction], device)
    each_row(side_products)
    far_arrived(1)
    for i in range(ROWS):
        arrived(z_in.at[i], zp_r.at[i])
        add(i, 2 * parity, [z_in[i, b] for b in range(PER)])
    far_mirrored(0)
    far_mirrored(1)
    each_row(far_lefts, lambda i: far_products(0, i), lambda i: far_products(1, i))
    for i in range(ROWS):
        arrived(x_in.at[i], xp_r.at[i])
        add(i, mine[2], [x_in[i, b] for b in range(PER)])
    for copy in sent:
        copy.wait_send()


def square_rows(density, block_cols):
    rows, nz, b, _ = density.shape
    f32, i32 = density.dtype, jnp.int32
    dma = pltpu.SemaphoreType.DMA
    anywhere = pl.BlockSpec(memory_space=pl.ANY)
    vmem, smem = pltpu.VMEM, pltpu.SMEM
    tables = [(rows, nz), (2, 2, rows, nz), (2, 2, rows, nz), (2, rows, nz)]
    return pl.pallas_call(
        square_kernel,
        out_shape=jax.ShapeDtypeStruct(density.shape, f32),
        in_specs=[anywhere, anywhere],
        out_specs=pl.BlockSpec(memory_space=pltpu.VMEM),
        scratch_shapes=[
            vmem((rows, nz + 1, b, b), f32), vmem((rows, nz + 1, b, b), f32),
            *[vmem((2, 2, rows, PER + 1, b, b), f32)] * 4,
            *[vmem((2, rows, PER + 1, b, b), f32)] * 2,
            *[vmem((2, PER, b, b), f32)] * 4,
            vmem((rows, b, 12 * b), jnp.bfloat16),
            *[vmem(shape, i32) for shape in tables], vmem((rows, nz), i32),
            smem((2, rows, nz), i32), *[smem(shape, i32) for shape in tables[1:]],
            smem((rows, nz), i32),
            dma((2, 7)), dma((2, 7)), dma((2, 3)), dma((2, 3)), dma((6,)), dma((6,)),
            dma((2,)), dma((2,)), dma((2, 3)), dma((2, 3)),
            dma((2, 7)), dma((2, 7)), dma((6,)), dma((6,)),
            dma((2,)), dma((2,)), dma((2,)), dma((2,)), dma((1,)), dma((1,)),
            dma((1,)), dma((1,)), dma((6,)), dma((6,)),
            dma((2,)), dma((2,)), dma((2,)), dma((2,)), dma((2,)), dma((6,)),
        ],
        compiler_params=pltpu.CompilerParams(
            collective_id=0, has_side_effects=True, vmem_limit_bytes=24 * 2**20),
    )(pltpu.with_memory_space_constraint(density, pltpu.HBM),
      pltpu.with_memory_space_constraint(block_cols, pltpu.HBM))


def shards(density, block_cols, targets):
    del targets
    return 2.0 * density - square_rows(density, block_cols)


def solution(mesh):
    return jax.shard_map(
        shards,
        mesh=mesh,
        in_specs=(
            P(("blk", "inner"), None, None, None),
            P(("blk", "inner"), None),
            P(("blk", "inner"), None, None),
        ),
        out_specs=P(("blk", "inner"), None, None, None),
        check_vma=False,
    )
```

time: 59.7 us -> 53.3 us (0.89)
  Pallas kernels: 57.1 us -> 52 us
  other arithmetic: 2.44 us -> 1.17 us
    pallas_call x1, Pallas kernels: 57.1 us -> 52 us  [square_rows(): pl.pallas_call(square_kernel, out_shape=jax.ShapeDtypeStruct(density.shap...]
    sub x1, other arithmetic: 2.44 us -> 1.17 us  [shards(): return 2.0 * density - square_rows(density, block_cols)]
where the time goes in v5:
time: 53.3 us; the launch traced here: 53.2 us
  Pallas kernels  52 us (98%)
  other arithmetic  1.17 us (2%)
    pallas_call x1, Pallas kernels, square_rows(): pl.pallas_call(square_kernel, out_shape=jax.ShapeDtypeStruct(density.shap...  52 us
    sub x1, other arithmetic, shards(): return 2.0 * density - square_rows(density, block_cols)  1.17 us

profile of v5, /device:TPU:1, one launch (start us, length us, event | category | flops | bytes accessed | tf_op | source)
XLA Modules:
  0.0 53.2 jit_solution(3549843041372670904)
XLA Ops:
  0.0 0.0 copy-start
  0.0 52.0 %shard_map.28 = f32[2,9,128,128]{3,2,1,0:T(8,128)S(1)} custom-call(f32[2,9,128,128]{3,2,1,0:T(8,128)} %den.1, s32[2,9]{1,0:T(2,128)} %cols.1), custom_call_target="tpu_custom_call" | custom-call | tf_op jit(solution)/shard_map/pallas_call | solution.py:407
  52.0 0.0 copy-done
  52.0 1.2 %multiply_subtract_fusion = f32[2,9,128,128]{3,2,1,0:T(8,128)} fusion(f32[2,9,128,128]{3,2,1,0:T(8,128)S(1)} %shard_map.28, f32[2,9,128,128]{3,2,1,0:T(8,128)S(1)} %copy-done), kind=kLoop, calls=%fused_computation | loop fusion | flops 589824 | bytes 3538944 | tf_op jit(solution)/shard_map/sub | solution.py:436
Async XLA Ops:
  0.0 52.0 %copy-start = (f32[2,9,128,128]{3,2,1,0:T(8,128)S(1)}, f32[2,9,128,128]{3,2,1,0:T(8,128)}, u32[]{:S(2)}) copy-start(f32[2,9,128,128]{3,2,1,0:T(8,128)} %den.1) | copy-start | bytes 3538948

commit v6 on v0

v6 whole, which is shorter than its diff:
```python
import jax
import jax.numpy as jnp
from jax import lax
from jax.experimental import pallas as pl
from jax.experimental.pallas import tpu as pltpu
from jax.sharding import PartitionSpec as P

MESH = pl.DeviceIdType.MESH
PER = 3
NZ = 9
X = 4
ROWS = 2


def split(value):
    high = value.astype(jnp.bfloat16)
    return high, (value - high.astype(jnp.float32)).astype(jnp.bfloat16)


def find(columns, wanted, places, otherwise):
    place = jnp.int32(otherwise)
    for column, here in zip(columns, places):
        place = jnp.where(column == wanted, here, place)
    return place


def left_side(blocks):
    highs, lows = zip(*(split(block.T) for block in blocks))
    return jnp.concatenate(highs + lows + highs, axis=1)


def right_side(columns_of_blocks):
    columns = []
    for blocks in columns_of_blocks:
        highs, lows = zip(*(split(block) for block in blocks))
        columns.append(jnp.concatenate(highs + highs + lows, axis=0))
    return jnp.concatenate(columns, axis=1)


def square_kernel(
    den, cols, out,
    own0, own1, p1, p2, q0, q1, d0, d1, f0, f1, p_out, p_in, q_out, q_in,
    c_own, c_p, c_q, c_d, c_f, t_own, t_p, t_q, t_d, t_f,
    send_s, recv_s, mirror_s, mirrored_s, own_s, own_r, table_send, table_recv,
    table_out, table_back, part_s, part_r, local_s, table_s,
):
    blk = lax.axis_index("blk")
    inner = lax.axis_index("inner")
    strips = lax.axis_size("blk")
    parity = lax.rem(blk, 2)
    core = lax.rem(inner, 2)
    chip_x = 2 * (inner // 2) + parity

    def at_x(x):
        x = lax.rem(x, X)
        return (blk - parity + lax.rem(x, 2), 2 * (x // 2) + core)

    p_chip = at_x(chip_x + 1 + 2 * parity)
    q_chip = at_x(chip_x + 3 - 2 * parity)
    mirror = (blk, inner + 1 - 2 * core)
    f_to = (lax.rem(blk + strips + 2 - 4 * parity, strips), inner)
    d_to = (lax.rem(blk + strips - 2 + 4 * parity, strips), inner)

    barrier = pltpu.get_barrier_semaphore()
    for device in (p_chip, q_chip, mirror, f_to, d_to):
        pl.semaphore_signal(barrier, inc=1, device_id=device, device_id_type=MESH)

    owned = []
    for row in range(ROWS):
        copy = pltpu.make_async_copy(den.at[row], own0.at[row, pl.ds(0, NZ)], local_s.at[row])
        copy.start()
        owned.append(copy)
    tables = [pltpu.make_async_copy(cols, t_own.at[0], table_s.at[0])]
    tables[0].start()

    none = jnp.zeros(den.shape[2:], jnp.float32)
    for row in range(ROWS):
        own0[row, NZ] = none
        own1[row, NZ] = none
        for half in range(2):
            for buffer in (p1, p2, q0, q1, d0, d1, f0, f1):
                buffer[half, row, PER] = none

    pl.semaphore_wait(barrier, 5)

    sent = []

    def send(src, dst, s, r, device):
        copy = pltpu.make_async_remote_copy(
            src_ref=src, dst_ref=dst, send_sem=s, recv_sem=r,
            device_id=device, device_id_type=MESH,
        )
        copy.start()
        sent.append(copy)

    def arrived(dst, r):
        pltpu.make_async_remote_copy(
            src_ref=dst, dst_ref=dst, send_sem=r, recv_sem=r,
            device_id=mirror, device_id_type=MESH,
        ).wait_recv()

    def groups(p):
        return (2 * p, 1, 2 - 2 * p)

    def slots(group):
        return pl.ds(PER * group, PER)

    mine = groups(parity)
    theirs = groups(1 - parity)

    P_FLOW, Q_FLOW, D_FLOW, F_FLOW = range(4)
    buffers = {P_FLOW: {1: p1, 2: p2}, Q_FLOW: {1: q1, 0: q0},
               D_FLOW: {0: d0, 1: d1}, F_FLOW: {1: f1, 0: f0}}
    order = {P_FLOW: (1, 2), Q_FLOW: (1, 0), D_FLOW: (0, 1), F_FLOW: (1, 0)}
    c_table = (c_p, c_q, c_d, c_f)
    t_table = (t_p, t_q, t_d, t_f)

    def piece(flow, half, g, row):
        return buffers[flow][g].at[half, row, pl.ds(0, PER)]

    def place(flow, g, row):
        return 2 * order[flow].index(g) + row

    for flow, device in ((P_FLOW, p_chip), (Q_FLOW, q_chip), (D_FLOW, d_to)):
        send(cols, c_table[flow].at[0], table_send.at[flow], table_recv.at[flow], device)
    for step in range(2):
        for row in range(ROWS):
            for flow, device in ((Q_FLOW, q_chip), (P_FLOW, p_chip), (D_FLOW, d_to)):
                g = order[flow][step]
                n = place(flow, g, row)
                send(den.at[row, slots(mine[g])], piece(flow, 0, g, row),
                     send_s.at[flow, n], recv_s.at[flow, n], device)
    send(cols, c_own, own_s.at[ROWS], own_r.at[ROWS], mirror)
    for row in range(ROWS):
        send(den.at[row], own1.at[row, pl.ds(0, NZ)], own_s.at[row], own_r.at[row], mirror)

    def load_table(k, src, dst):
        copy = pltpu.make_async_copy(src, dst, table_s.at[k])
        copy.start()
        tables.append(copy)

    def flow_arrived(flow, step, row):
        g = order[flow][step]
        n = place(flow, g, row)
        arrived(piece(flow, 0, g, row), recv_s.at[flow, n])
        if flow == Q_FLOW:
            m = place(F_FLOW, g, row)
            send(piece(flow, 0, g, row), piece(F_FLOW, 0, g, row),
                 send_s.at[F_FLOW, m], recv_s.at[F_FLOW, m], f_to)
        send(piece(flow, 0, g, row), piece(flow, 1, g, row),
             mirror_s.at[flow, n], mirrored_s.at[flow, n], mirror)

    def mirrored(flow, g):
        for row in range(ROWS):
            arrived(piece(flow, 1, g, row), mirrored_s.at[flow, place(flow, g, row)])

    def table_arrived(flow):
        arrived(c_table[flow].at[0], table_recv.at[flow])
        if flow == Q_FLOW:
            send(c_q.at[0], c_f.at[0], table_send.at[F_FLOW], table_recv.at[F_FLOW], f_to)
        send(c_table[flow].at[0], c_table[flow].at[1], table_out.at[flow],
             table_back.at[flow], mirror)

    def first_of(device):
        return device[0] * (4 * ROWS) + device[1] * ROWS

    first, p_first, q_first = first_of((blk, inner)), first_of(p_chip), first_of(q_chip)

    def parts(lhs, rhs):
        product = jnp.dot(lhs, rhs, preferred_element_type=jnp.float32)
        width = den.shape[3]
        return [product[:, b * width:(b + 1) * width] for b in range(PER)]

    def entries(table, index, group):
        return [table[(*index, PER * group + b)] for b in range(PER)]

    def add(i, group, blocks, fresh=False):
        for b, block in enumerate(blocks):
            if fresh:
                out[i, PER * group + b] = block
            else:
                out[i, PER * group + b] += block

    pair = [(half, row) for half in range(2) for row in range(ROWS)]

    def products(target, left, wanted):
        names, reads = left
        lhs = left_side([read(find(name, target, range(PER), 0))
                         for name, read in zip(names, reads)])
        present = [find(name, target, (1, 1, 1), 0) == 1 for name in names]
        for (columns, blocks), want in wanted:
            columns = [[jnp.where(there, c, -1) for c in row]
                       for there, row in zip(present, columns)]
            rhs = right_side([
                [read(find(row, column, range(PER), empty))
                 for row, (read, empty) in zip(columns, blocks)]
                for column in want
            ])
            yield parts(lhs, rhs)

    def of_flow(flow, g, parity_there):
        buffer = buffers[flow][g]
        names = [entries(t_table[flow], index, groups(parity_there)[g]) for index in pair]
        reads = [lambda s, index=index: buffer[(*index, s)] for index in pair]
        return names, reads

    def right_of_flow(flow, g, parity_there):
        names, reads = of_flow(flow, g, parity_there)
        return names, [(read, PER) for read in reads]

    def of_own(group):
        names = [entries(t_own, index, group) for index in pair]
        reads = [lambda s, buffer=(own0, own1)[half], row=row: buffer[row, PER * group + s]
                 for half, row in pair]
        return names, reads

    def right_of_own(group):
        names, reads = of_own(group)
        return names, [(read, NZ - PER * group) for read in reads]

    def want(i, group):
        return entries(t_own, (0, i), group)

    def own_products(i):
        for e, blocks in enumerate(products(
                first + i, of_own(1), [(right_of_own(e), want(i, e)) for e in range(3)])):
            add(i, e, blocks, fresh=True)

    def store(ref, k, i, blocks, fresh=False):
        for b, block in enumerate(blocks):
            if fresh:
                ref[k, i, b] = block
            else:
                ref[k, i, b] += block

    def q_own(i):
        wanted = [(right_of_own(mine[2]), entries(t_q, (0, i), 1)),
                  (right_of_own(1), entries(t_q, (0, i), theirs[2]))]
        for k, blocks in enumerate(products(q_first + i, of_own(mine[2]), wanted)):
            store(q_out, k, i, blocks, fresh=True)

    def q_part(k, i):
        g = (1, 2)[k]
        (blocks,) = products(q_first + i, of_flow(P_FLOW, 1, 1 - parity), [
            (right_of_flow(P_FLOW, g, 1 - parity), entries(t_q, (0, i), theirs[g]))])
        store(q_out, k, i, blocks)

    def p_part(k, i):
        g = (0, 1)[k]
        (blocks,) = products(p_first + i, of_flow(D_FLOW, 0, parity), [
            (right_of_flow(D_FLOW, g, parity), entries(t_p, (0, i), theirs[(1, 0)[k]]))])
        store(p_out, k, i, blocks, fresh=True)

    def p_part_q(i):
        (blocks,) = products(p_first + i, of_flow(Q_FLOW, 1, 1 - parity), [
            (right_of_flow(Q_FLOW, 0, 1 - parity), entries(t_p, (0, i), theirs[0]))])
        store(p_out, 1, i, blocks)

    def from_p(i):
        wanted = [(right_of_flow(P_FLOW, 2, 1 - parity), want(i, 1)),
                  (right_of_flow(P_FLOW, 1, 1 - parity), want(i, mine[2]))]
        for group, blocks in zip((1, mine[2]), products(
                first + i, of_flow(P_FLOW, 2, 1 - parity), wanted)):
            add(i, group, blocks)

    def from_f(i):
        wanted = [(right_of_flow(F_FLOW, 0, 1 - parity), want(i, 1)),
                  (right_of_flow(F_FLOW, 1, 1 - parity), want(i, mine[0]))]
        for group, blocks in zip((1, mine[0]), products(
                first + i, of_flow(F_FLOW, 0, 1 - parity), wanted)):
            add(i, group, blocks)

    def each_row(*steps):
        def body(i, carry):
            for step in steps:
                step(i)
            return carry
        lax.fori_loop(0, ROWS, body, 0)

    def send_part(k, i):
        for n, (src, dst, device) in enumerate(((q_out, q_in, q_chip), (p_out, p_in, p_chip))):
            send(src.at[k, i], dst.at[k, i], part_s.at[n, 2 * k + i], part_r.at[n, 2 * k + i],
                 device)

    def part_arrived(k, i):
        for n, (ref, group) in enumerate(((q_in, (1, mine[2])[k]), (p_in, (1, mine[0])[k]))):
            arrived(ref.at[k, i], part_r.at[n, 2 * k + i])
            add(i, group, [ref[k, i, b] for b in range(PER)])

    raw = (Q_FLOW, P_FLOW, D_FLOW)
    for flow in raw:
        table_arrived(flow)
    arrived(c_own, own_r.at[ROWS])
    load_table(1, c_own, t_own.at[1])
    for copy in owned:
        copy.wait()
    for row in range(ROWS):
        arrived(own1.at[row, pl.ds(0, NZ)], own_r.at[row])
    for k in range(2):
        tables[k].wait()
    each_row(own_products)
    table_arrived(F_FLOW)
    for flow in raw:
        flow_arrived(flow, 0, 0)
    for flow in (*raw, F_FLOW):
        arrived(c_table[flow].at[1], table_back.at[flow])
        load_table(2 + flow, c_table[flow], t_table[flow])
    for k in range(2, 6):
        tables[k].wait()
    each_row(q_own)
    for flow in raw:
        flow_arrived(flow, 0, 1)
    flow_arrived(F_FLOW, 0, 0)
    mirrored(P_FLOW, 1)
    mirrored(D_FLOW, 0)
    mirrored(Q_FLOW, 1)
    each_row(lambda i: q_part(0, i), lambda i: p_part(0, i))
    for flow in raw:
        flow_arrived(flow, 1, 0)
    for i in range(ROWS):
        send_part(0, i)
    flow_arrived(F_FLOW, 0, 1)
    for flow in raw:
        flow_arrived(flow, 1, 1)
    mirrored(P_FLOW, 2)
    mirrored(D_FLOW, 1)
    mirrored(Q_FLOW, 0)
    for i in range(ROWS):
        q_part(1, i)
        p_part(1, i)
        p_part_q(i)
        send_part(1, i)
    flow_arrived(F_FLOW, 1, 0)
    flow_arrived(F_FLOW, 1, 1)
    each_row(from_p)
    mirrored(F_FLOW, 1)
    mirrored(F_FLOW, 0)
    each_row(from_f)
    for k in range(2):
        for i in range(ROWS):
            part_arrived(k, i)
    for copy in sent:
        copy.wait_send()


def square_rows(density, block_cols):
    rows, nz, b, _ = density.shape
    f32, i32 = density.dtype, jnp.int32
    dma = pltpu.SemaphoreType.DMA
    anywhere = pl.BlockSpec(memory_space=pl.ANY)
    vmem, smem = pltpu.VMEM, pltpu.SMEM
    return pl.pallas_call(
        square_kernel,
        out_shape=jax.ShapeDtypeStruct(density.shape, f32),
        in_specs=[anywhere, anywhere],
        out_specs=pl.BlockSpec(memory_space=pltpu.VMEM),
        scratch_shapes=[
            *[vmem((rows, nz + 1, b, b), f32)] * 2,
            *[vmem((2, rows, PER + 1, b, b), f32)] * 8,
            *[vmem((2, rows, PER, b, b), f32)] * 4,
            vmem((rows, nz), i32), *[vmem((2, rows, nz), i32)] * 4,
            *[smem((2, rows, nz), i32)] * 5,
            dma((4, 4)), dma((4, 4)), dma((4, 4)), dma((4, 4)),
            dma((3,)), dma((3,)), dma((4,)), dma((4,)), dma((4,)), dma((4,)),
            dma((2, 4)), dma((2, 4)), dma((2,)), dma((6,)),
        ],
        compiler_params=pltpu.CompilerParams(
            collective_id=0, has_side_effects=True, vmem_limit_bytes=24 * 2**20),
    )(pltpu.with_memory_space_constraint(density, pltpu.HBM),
      pltpu.with_memory_space_constraint(block_cols, pltpu.HBM))


def shards(density, block_cols, targets):
    del targets
    return 2.0 * density - square_rows(density, block_cols)


def solution(mesh):
    return jax.shard_map(
        shards,
        mesh=mesh,
        in_specs=(
            P(("blk", "inner"), None, None, None),
            P(("blk", "inner"), None),
            P(("blk", "inner"), None, None),
        ),
        out_specs=P(("blk", "inner"), None, None, None),
        check_vma=False,
    )
```

time: 322 us -> 47.8 us (0.15)
  waiting for transfers between devices: 209 us -> 0 us
  other arithmetic: 53 us -> 1.17 us
  Pallas kernels: 0 us -> 46.5 us
  local copies, waits for them, and re-layouts: 22.2 us -> 0.01 us
  matrix products: 13.9 us -> 0 us
  between operations: 13.4 us -> 0.02 us
  starting transfers between devices: 10.3 us -> 0 us
    ppermute x2 -> x0, waiting for transfers between devices: 149 us -> none  [shifted(): return lax.ppermute(value, axis, pairs)]
    reduce_scatter x1 -> x0, waiting for transfers between devices: 60.1 us -> none  [shards(): square = lax.psum_scatter(total, 'inner', scatter_dimension=0, tiled=True)]
    pallas_call x0 -> x1, Pallas kernels: none -> 46.5 us  [square_rows(): pl.pallas_call(square_kernel, out_shape=jax.ShapeDtypeStruct(density.shap...]
    scatter-add x3 -> x0, other arithmetic: 39.6 us -> none  [panel_lookup(): panel.at[cells.reshape(-1)]]
    dot_general x3 -> x0, matrix products: 13.9 us -> none  [panel_lookup(): jnp.einsum('kmab,ktac->kmtbc', sources, density, precision=lax.Precision....]
    transpose x3 -> x0, local copies, waits for them, and re-layouts: 13.3 us -> none  [panel_lookup(): jnp.einsum('kmab,ktac->kmtbc', sources, density, precision=lax.Precision....]
    ppermute x2 -> x0, starting transfers between devices: 10.3 us -> none  [shifted(): return lax.ppermute(value, axis, pairs)]
    add x1 -> x0, other arithmetic: 9.34 us -> none  [shards(): total = total.at[:, lower_low:lower_upper_bound].add(from_above)]
  transfers between devices with their start and end apart: 3 -> 0, of which waited for: 3 -> 0; matrix products, arithmetic and copies ran while one was open for 16% -> 0% of each run, Pallas kernels for 0% -> 0%
where the time goes in v6:
time: 47.8 us; the launch traced here: 47.7 us
  Pallas kernels  46.5 us (97%)
  other arithmetic  1.17 us (2%)
    pallas_call x1, Pallas kernels, square_rows(): pl.pallas_call(square_kernel, out_shape=jax.ShapeDtypeStruct(density.shap...  46.5 us
    sub x1, other arithmetic, shards(): return 2.0 * density - square_rows(density, block_cols)  1.17 us

profile of v6, /device:TPU:1, one launch (start us, length us, event | category | flops | bytes accessed | tf_op | source)
XLA Modules:
  0.0 47.7 jit_solution(10671354798420082472)
XLA Ops:
  0.0 0.0 copy-start
  0.0 46.5 %shard_map.28 = f32[2,9,128,128]{3,2,1,0:T(8,128)S(1)} custom-call(f32[2,9,128,128]{3,2,1,0:T(8,128)} %den.1, s32[2,9]{1,0:T(2,128)} %cols.1), custom_call_target="tpu_custom_call" | custom-call | tf_op jit(solution)/shard_map/pallas_call | solution.py:352
  46.5 0.0 copy-done
  46.5 1.2 %multiply_subtract_fusion = f32[2,9,128,128]{3,2,1,0:T(8,128)} fusion(f32[2,9,128,128]{3,2,1,0:T(8,128)S(1)} %shard_map.28, f32[2,9,128,128]{3,2,1,0:T(8,128)S(1)} %copy-done), kind=kLoop, calls=%fused_computation | loop fusion | flops 589824 | bytes 3538944 | tf_op jit(solution)/shard_map/sub | solution.py:375
Async XLA Ops:
  0.0 46.5 %copy-start = (f32[2,9,128,128]{3,2,1,0:T(8,128)S(1)}, f32[2,9,128,128]{3,2,1,0:T(8,128)}, u32[]{:S(2)}) copy-start(f32[2,9,128,128]{3,2,1,0:T(8,128)} %den.1) | copy-start | bytes 3538948

commit v7 on v6

--- a/solution.py
+++ b/solution.py
@@ -62,7 +62,7 @@
     d_to = (lax.rem(blk + strips - 2 + 4 * parity, strips), inner)
 
     barrier = pltpu.get_barrier_semaphore()
-    for device in (p_chip, q_chip, mirror, f_to, d_to):
+    for device in (p_chip, q_chip, mirror):
         pl.semaphore_signal(barrier, inc=1, device_id=device, device_id_type=MESH)
 
     owned = []
@@ -81,7 +81,18 @@
             for buffer in (p1, p2, q0, q1, d0, d1, f0, f1):
                 buffer[half, row, PER] = none
 
-    pl.semaphore_wait(barrier, 5)
+    even_z = lax.rem(blk // 2, 2) == 0
+
+    @pl.when(even_z)
+    def _():
+        pl.semaphore_wait(barrier, 3)
+
+    @pl.when(jnp.logical_not(even_z))
+    def _():
+        pl.semaphore_wait(barrier, 5)
+
+    for device in (f_to, d_to):
+        pl.semaphore_signal(barrier, inc=1, device_id=device, device_id_type=MESH)
 
     sent = []
 
@@ -121,18 +132,27 @@
     def place(flow, g, row):
         return 2 * order[flow].index(g) + row
 
-    for flow, device in ((P_FLOW, p_chip), (Q_FLOW, q_chip), (D_FLOW, d_to)):
-        send(cols, c_table[flow].at[0], table_send.at[flow], table_recv.at[flow], device)
-    for step in range(2):
-        for row in range(ROWS):
-            for flow, device in ((Q_FLOW, q_chip), (P_FLOW, p_chip), (D_FLOW, d_to)):
-                g = order[flow][step]
-                n = place(flow, g, row)
-                send(den.at[row, slots(mine[g])], piece(flow, 0, g, row),
-                     send_s.at[flow, n], recv_s.at[flow, n], device)
+    def send_flows(*flows):
+        for flow, device in flows:
+            send(cols, c_table[flow].at[0], table_send.at[flow], table_recv.at[flow], device)
+        for step in range(2):
+            for row in range(ROWS):
+                for flow, device in flows:
+                    g = order[flow][step]
+                    n = place(flow, g, row)
+                    send(den.at[row, slots(mine[g])], piece(flow, 0, g, row),
+                         send_s.at[flow, n], recv_s.at[flow, n], device)
+
+    send_flows((Q_FLOW, q_chip), (P_FLOW, p_chip))
     send(cols, c_own, own_s.at[ROWS], own_r.at[ROWS], mirror)
     for row in range(ROWS):
         send(den.at[row], own1.at[row, pl.ds(0, NZ)], own_s.at[row], own_r.at[row], mirror)
+
+    @pl.when(even_z)
+    def _():
+        pl.semaphore_wait(barrier, 2)
+
+    send_flows((D_FLOW, d_to))
 
     def load_table(k, src, dst):
         copy = pltpu.make_async_copy(src, dst, table_s.at[k])

time: 47.8 us -> 46.1 us (0.964); the launches traced: 47.7 us -> 45.3 us
  Pallas kernels: 46.5 us -> 44.1 us
    pallas_call x1, Pallas kernels: 46.5 us -> 44.1 us  [square_rows(): pl.pallas_call(square_kernel, out_shape=jax.ShapeDtypeStruct(density.shap...]
where the time goes in v7:
time: 46.1 us; the launch traced here: 45.3 us
  Pallas kernels  44.1 us (96%)
  other arithmetic  1.17 us (3%)
    pallas_call x1, Pallas kernels, square_rows(): pl.pallas_call(square_kernel, out_shape=jax.ShapeDtypeStruct(density.shap...  44.1 us
    sub x1, other arithmetic, shards(): return 2.0 * density - square_rows(density, block_cols)  1.17 us

profile of v7, /device:TPU:1, one launch (start us, length us, event | category | flops | bytes accessed | tf_op | source)
XLA Modules:
  0.0 45.3 jit_solution(5784129457706608639)
XLA Ops:
  0.0 0.0 copy-start
  0.0 44.1 %shard_map.28 = f32[2,9,128,128]{3,2,1,0:T(8,128)S(1)} custom-call(f32[2,9,128,128]{3,2,1,0:T(8,128)} %den.1, s32[2,9]{1,0:T(2,128)} %cols.1), custom_call_target="tpu_custom_call" | custom-call | tf_op jit(solution)/shard_map/pallas_call | solution.py:372
  44.1 0.0 copy-done
  44.1 1.2 %multiply_subtract_fusion = f32[2,9,128,128]{3,2,1,0:T(8,128)} fusion(f32[2,9,128,128]{3,2,1,0:T(8,128)S(1)} %shard_map.28, f32[2,9,128,128]{3,2,1,0:T(8,128)S(1)} %copy-done), kind=kLoop, calls=%fused_computation | loop fusion | flops 589824 | bytes 3538944 | tf_op jit(solution)/shard_map/sub | solution.py:395
Async XLA Ops:
  0.0 44.1 %copy-start = (f32[2,9,128,128]{3,2,1,0:T(8,128)S(1)}, f32[2,9,128,128]{3,2,1,0:T(8,128)}, u32[]{:S(2)}) copy-start(f32[2,9,128,128]{3,2,1,0:T(8,128)} %den.1) | copy-start | bytes 3538948

commit v8 on v7

--- a/solution.py
+++ b/solution.py
@@ -9,6 +9,7 @@
 PER = 3
 NZ = 9
 X = 4
+Z = 8
 ROWS = 2
 
 
@@ -37,7 +38,7 @@
     return jnp.concatenate(columns, axis=1)
 
 
-def square_kernel(
+def purify_kernel(
     den, cols, out,
     own0, own1, p1, p2, q0, q1, d0, d1, f0, f1, p_out, p_in, q_out, q_in,
     c_own, c_p, c_q, c_d, c_f, t_own, t_p, t_q, t_d, t_f,
@@ -197,9 +198,9 @@
     def add(i, group, blocks, fresh=False):
         for b, block in enumerate(blocks):
             if fresh:
-                out[i, PER * group + b] = block
+                out[i, PER * group + b] = 2.0 * own0[i, PER * group + b] - block
             else:
-                out[i, PER * group + b] += block
+                out[i, PER * group + b] -= block
 
     pair = [(half, row) for half in range(2) for row in range(ROWS)]
 
@@ -269,12 +270,12 @@
         g = (0, 1)[k]
         (blocks,) = products(p_first + i, of_flow(D_FLOW, 0, parity), [
             (right_of_flow(D_FLOW, g, parity), entries(t_p, (0, i), theirs[(1, 0)[k]]))])
-        store(p_out, k, i, blocks, fresh=True)
+        store(p_out, k, i, blocks, fresh=k == 0)
 
     def p_part_q(i):
         (blocks,) = products(p_first + i, of_flow(Q_FLOW, 1, 1 - parity), [
             (right_of_flow(Q_FLOW, 0, 1 - parity), entries(t_p, (0, i), theirs[0]))])
-        store(p_out, 1, i, blocks)
+        store(p_out, 1, i, blocks, fresh=True)
 
     def from_p(i):
         wanted = [(right_of_flow(P_FLOW, 2, 1 - parity), want(i, 1)),
@@ -297,19 +298,25 @@
             return carry
         lax.fori_loop(0, ROWS, body, 0)
 
-    def send_part(k, i):
-        for n, (src, dst, device) in enumerate(((q_out, q_in, q_chip), (p_out, p_in, p_chip))):
-            send(src.at[k, i], dst.at[k, i], part_s.at[n, 2 * k + i], part_r.at[n, 2 * k + i],
-                 device)
+    def send_part(n, k, i):
+        src, dst, device = ((q_out, q_in, q_chip), (p_out, p_in, p_chip))[n]
+        send(src.at[k, i], dst.at[k, i], part_s.at[n, 2 * k + i], part_r.at[n, 2 * k + i],
+             device)
 
     def part_arrived(k, i):
         for n, (ref, group) in enumerate(((q_in, (1, mine[2])[k]), (p_in, (1, mine[0])[k]))):
             arrived(ref.at[k, i], part_r.at[n, 2 * k + i])
             add(i, group, [ref[k, i, b] for b in range(PER)])
 
-    raw = (Q_FLOW, P_FLOW, D_FLOW)
-    for flow in raw:
-        table_arrived(flow)
+    def tables_ready(*flows):
+        for flow in flows:
+            arrived(c_table[flow].at[1], table_back.at[flow])
+            load_table(2 + flow, c_table[flow], t_table[flow])
+        for copy in tables[-len(flows):]:
+            copy.wait()
+
+    table_arrived(Q_FLOW)
+    table_arrived(P_FLOW)
     arrived(c_own, own_r.at[ROWS])
     load_table(1, c_own, t_own.at[1])
     for copy in owned:
@@ -319,37 +326,44 @@
     for k in range(2):
         tables[k].wait()
     each_row(own_products)
+    flow_arrived(Q_FLOW, 0, 0)
+    flow_arrived(P_FLOW, 0, 0)
+    tables_ready(P_FLOW, Q_FLOW)
+    each_row(q_own)
+    flow_arrived(Q_FLOW, 0, 1)
+    flow_arrived(P_FLOW, 0, 1)
+    mirrored(P_FLOW, 1)
+    each_row(lambda i: q_part(0, i))
+    table_arrived(D_FLOW)
     table_arrived(F_FLOW)
-    for flow in raw:
-        flow_arrived(flow, 0, 0)
-    for flow in (*raw, F_FLOW):
-        arrived(c_table[flow].at[1], table_back.at[flow])
-        load_table(2 + flow, c_table[flow], t_table[flow])
-    for k in range(2, 6):
-        tables[k].wait()
-    each_row(q_own)
-    for flow in raw:
-        flow_arrived(flow, 0, 1)
+    flow_arrived(D_FLOW, 0, 0)
+    flow_arrived(D_FLOW, 0, 1)
+    for i in range(ROWS):
+        send_part(0, 0, i)
+    flow_arrived(Q_FLOW, 1, 0)
+    flow_arrived(P_FLOW, 1, 0)
+    tables_ready(D_FLOW, F_FLOW)
+    mirrored(D_FLOW, 0)
+    each_row(lambda i: p_part(0, i))
     flow_arrived(F_FLOW, 0, 0)
-    mirrored(P_FLOW, 1)
-    mirrored(D_FLOW, 0)
+    for i in range(ROWS):
+        send_part(1, 0, i)
+    flow_arrived(Q_FLOW, 1, 1)
+    flow_arrived(P_FLOW, 1, 1)
     mirrored(Q_FLOW, 1)
-    each_row(lambda i: q_part(0, i), lambda i: p_part(0, i))
-    for flow in raw:
-        flow_arrived(flow, 1, 0)
-    for i in range(ROWS):
-        send_part(0, i)
-    flow_arrived(F_FLOW, 0, 1)
-    for flow in raw:
-        flow_arrived(flow, 1, 1)
     mirrored(P_FLOW, 2)
-    mirrored(D_FLOW, 1)
-    mirrored(Q_FLOW, 0)
+    flow_arrived(D_FLOW, 1, 0)
     for i in range(ROWS):
         q_part(1, i)
+        send_part(0, 1, i)
+    flow_arrived(D_FLOW, 1, 1)
+    mirrored(Q_FLOW, 0)
+    each_row(p_part_q)
+    mirrored(D_FLOW, 1)
+    for i in range(ROWS):
         p_part(1, i)
-        p_part_q(i)
-        send_part(1, i)
+        send_part(1, 1, i)
+    flow_arrived(F_FLOW, 0, 1)
     flow_arrived(F_FLOW, 1, 0)
     flow_arrived(F_FLOW, 1, 1)
     each_row(from_p)
@@ -363,14 +377,14 @@
         copy.wait_send()
 
 
-def square_rows(density, block_cols):
+def purified_rows(density, block_cols):
     rows, nz, b, _ = density.shape
     f32, i32 = density.dtype, jnp.int32
     dma = pltpu.SemaphoreType.DMA
     anywhere = pl.BlockSpec(memory_space=pl.ANY)
     vmem, smem = pltpu.VMEM, pltpu.SMEM
     return pl.pallas_call(
-        square_kernel,
+        purify_kernel,
         out_shape=jax.ShapeDtypeStruct(density.shape, f32),
         in_specs=[anywhere, anywhere],
         out_specs=pl.BlockSpec(memory_space=pltpu.VMEM),
@@ -392,7 +406,7 @@
 
 def shards(density, block_cols, targets):
     del targets
-    return 2.0 * density - square_rows(density, block_cols)
+    return purified_rows(density, block_cols)
 
 
 def solution(mesh):

time: 46.1 us -> 45.6 us (0.989); the launches traced: 45.3 us -> 45.5 us
  other arithmetic: 1.17 us -> 0 us
  local copies, waits for them, and re-layouts: 0.01 us -> 1.02 us
    sub x1 -> x0, other arithmetic: 1.17 us -> none  [shards(): return 2.0 * density - square_rows(density, block_cols)]
    unnamed x2 -> x1, local copies, waits for them, and re-layouts: 0.01 us -> 1.02 us
where the time goes in v8:
time: 45.6 us; the launch traced here: 45.5 us
  Pallas kernels  44.5 us (98%)
  local copies, waits for them, and re-layouts  1.02 us (2%)
    pallas_call x1, Pallas kernels, purified_rows(): pl.pallas_call(purify_kernel, out_shape=jax.ShapeDtypeStruct(density.shap...  44.5 us
    unnamed x1, local copies, waits for them, and re-layouts  1.02 us

profile of v8, /device:TPU:1, one launch (start us, length us, event | category | flops | bytes accessed | tf_op | source)
XLA Modules:
  0.0 45.5 jit_solution(2528168698008076177)
XLA Ops:
  0.0 44.5 %shard_map.28 = f32[2,9,128,128]{3,2,1,0:T(8,128)S(1)} custom-call(f32[2,9,128,128]{3,2,1,0:T(8,128)} %den.1, s32[2,9]{1,0:T(2,128)} %cols.1), custom_call_target="tpu_custom_call" | custom-call | tf_op jit(solution)/shard_map/pallas_call | solution.py:386
  44.5 1.0 %copy.4 = f32[2,9,128,128]{3,2,1,0:T(8,128)} copy(f32[2,9,128,128]{3,2,1,0:T(8,128)S(1)} %shard_map.28) | data formatting | bytes 2359296

commit v9 on v8

--- a/solution.py
+++ b/solution.py
@@ -9,6 +9,7 @@
 PER = 3
 NZ = 9
 X = 4
+Z = 8
 Z = 8
 ROWS = 2
 
@@ -82,28 +83,29 @@
             for buffer in (p1, p2, q0, q1, d0, d1, f0, f1):
                 buffer[half, row, PER] = none
 
-    even_z = lax.rem(blk // 2, 2) == 0
-
-    @pl.when(even_z)
-    def _():
-        pl.semaphore_wait(barrier, 3)
-
-    @pl.when(jnp.logical_not(even_z))
-    def _():
-        pl.semaphore_wait(barrier, 5)
+    plane = lax.rem(blk // 2, Z)
+    early = (plane == 0) | (plane == 3) | (plane == 5)
+    middle = (plane == 1) | (plane == 7)
+    late = jnp.logical_not(early | middle)
+    for when, before in ((early, 0), (middle, 1), (late, 2)):
+        @pl.when(when)
+        def _(count=3 + before):
+            pl.semaphore_wait(barrier, count)
 
     for device in (f_to, d_to):
         pl.semaphore_signal(barrier, inc=1, device_id=device, device_id_type=MESH)
 
     sent = []
 
-    def send(src, dst, s, r, device):
+    def send(src, dst, s, r, device, start=True, record=True):
         copy = pltpu.make_async_remote_copy(
             src_ref=src, dst_ref=dst, send_sem=s, recv_sem=r,
             device_id=device, device_id_type=MESH,
         )
-        copy.start()
-        sent.append(copy)
+        if start:
+            copy.start()
+        if record:
+            sent.append(copy)
 
     def arrived(dst, r):
         pltpu.make_async_remote_copy(
@@ -133,27 +135,38 @@
     def place(flow, g, row):
         return 2 * order[flow].index(g) + row
 
-    def send_flows(*flows):
+    def send_flows(*flows, **what):
         for flow, device in flows:
-            send(cols, c_table[flow].at[0], table_send.at[flow], table_recv.at[flow], device)
+            send(cols, c_table[flow].at[0], table_send.at[flow], table_recv.at[flow], device, **what)
         for step in range(2):
             for row in range(ROWS):
                 for flow, device in flows:
                     g = order[flow][step]
                     n = place(flow, g, row)
                     send(den.at[row, slots(mine[g])], piece(flow, 0, g, row),
-                         send_s.at[flow, n], recv_s.at[flow, n], device)
+                         send_s.at[flow, n], recv_s.at[flow, n], device, **what)
 
     send_flows((Q_FLOW, q_chip), (P_FLOW, p_chip))
     send(cols, c_own, own_s.at[ROWS], own_r.at[ROWS], mirror)
     for row in range(ROWS):
         send(den.at[row], own1.at[row, pl.ds(0, NZ)], own_s.at[row], own_r.at[row], mirror)
 
-    @pl.when(even_z)
+    known = late | (middle & ((plane == 1) == (parity == 0)))
+
+    @pl.when(known)
     def _():
-        pl.semaphore_wait(barrier, 2)
-
-    send_flows((D_FLOW, d_to))
+        send_flows((D_FLOW, d_to), record=False)
+
+    for when, after in ((early, 2), (middle, 1)):
+        @pl.when(when)
+        def _(count=after):
+            pl.semaphore_wait(barrier, count)
+
+    @pl.when(jnp.logical_not(known))
+    def _():
+        send_flows((D_FLOW, d_to), record=False)
+
+    send_flows((D_FLOW, d_to), start=False)
 
     def load_table(k, src, dst):
         copy = pltpu.make_async_copy(src, dst, table_s.at[k])

time: 45.6 us -> 44.6 us (0.978)
  Pallas kernels: 44.5 us -> 43.5 us
    pallas_call x1, Pallas kernels: 44.5 us -> 43.5 us  [purified_rows(): pl.pallas_call(purify_kernel, out_shape=jax.ShapeDtypeStruct(density.shap...]
where the time goes in v9:
time: 44.6 us; the launch traced here: 44.5 us
  Pallas kernels  43.5 us (98%)
  local copies, waits for them, and re-layouts  1.02 us (2%)
    pallas_call x1, Pallas kernels, purified_rows(): pl.pallas_call(purify_kernel, out_shape=jax.ShapeDtypeStruct(density.shap...  43.5 us
    unnamed x1, local copies, waits for them, and re-layouts  1.02 us

profile of v9, /device:TPU:1, one launch (start us, length us, event | category | flops | bytes accessed | tf_op | source)
XLA Modules:
  0.0 44.5 jit_solution(8786371276031424431)
XLA Ops:
  0.0 43.5 %shard_map.28 = f32[2,9,128,128]{3,2,1,0:T(8,128)S(1)} custom-call(f32[2,9,128,128]{3,2,1,0:T(8,128)} %den.1, s32[2,9]{1,0:T(2,128)} %cols.1), custom_call_target="tpu_custom_call" | custom-call | tf_op jit(solution)/shard_map/pallas_call | solution.py:399
  43.5 1.0 %copy.4 = f32[2,9,128,128]{3,2,1,0:T(8,128)} copy(f32[2,9,128,128]{3,2,1,0:T(8,128)S(1)} %shard_map.28) | data formatting | bytes 2359296

commit v10 on v9

--- a/solution.py
+++ b/solution.py
@@ -41,7 +41,7 @@
 
 def purify_kernel(
     den, cols, out,
-    own0, own1, p1, p2, q0, q1, d0, d1, f0, f1, p_out, p_in, q_out, q_in,
+    own0, own1, p1, p2, q0, q1, d0, d1, d1_far, f0, f1, p_out, p_in, q_out, q_in,
     c_own, c_p, c_q, c_d, c_f, t_own, t_p, t_q, t_d, t_f,
     send_s, recv_s, mirror_s, mirrored_s, own_s, own_r, table_send, table_recv,
     table_out, table_back, part_s, part_r, local_s, table_s,
@@ -80,8 +80,9 @@
         own0[row, NZ] = none
         own1[row, NZ] = none
         for half in range(2):
-            for buffer in (p1, p2, q0, q1, d0, d1, f0, f1):
+            for buffer in (p1, p2, q0, q1, d0, f0, f1):
                 buffer[half, row, PER] = none
+            (d1, d1_far)[half][row, PER] = none
 
     plane = lax.rem(blk // 2, Z)
     early = (plane == 0) | (plane == 3) | (plane == 5)
@@ -124,13 +125,16 @@
 
     P_FLOW, Q_FLOW, D_FLOW, F_FLOW = range(4)
     buffers = {P_FLOW: {1: p1, 2: p2}, Q_FLOW: {1: q1, 0: q0},
-               D_FLOW: {0: d0, 1: d1}, F_FLOW: {1: f1, 0: f0}}
+               D_FLOW: {0: d0, 1: (d1, d1_far)}, F_FLOW: {1: f1, 0: f0}}
     order = {P_FLOW: (1, 2), Q_FLOW: (1, 0), D_FLOW: (0, 1), F_FLOW: (1, 0)}
     c_table = (c_p, c_q, c_d, c_f)
     t_table = (t_p, t_q, t_d, t_f)
 
     def piece(flow, half, g, row):
-        return buffers[flow][g].at[half, row, pl.ds(0, PER)]
+        buffer = buffers[flow][g]
+        if isinstance(buffer, tuple):
+            return buffer[half].at[row, pl.ds(0, PER)]
+        return buffer.at[half, row, pl.ds(0, PER)]
 
     def place(flow, g, row):
         return 2 * order[flow].index(g) + row
@@ -232,14 +236,17 @@
             ])
             yield parts(lhs, rhs)
 
-    def of_flow(flow, g, parity_there):
+    def of_flow(flow, g, parity_there, where=pair):
         buffer = buffers[flow][g]
-        names = [entries(t_table[flow], index, groups(parity_there)[g]) for index in pair]
-        reads = [lambda s, index=index: buffer[(*index, s)] for index in pair]
+        names = [entries(t_table[flow], index, groups(parity_there)[g]) for index in where]
+        if isinstance(buffer, tuple):
+            reads = [lambda s, half=half, row=row: buffer[half][row, s] for half, row in where]
+        else:
+            reads = [lambda s, index=index: buffer[(*index, s)] for index in where]
         return names, reads
 
-    def right_of_flow(flow, g, parity_there):
-        names, reads = of_flow(flow, g, parity_there)
+    def right_of_flow(flow, g, parity_there, where=pair):
+        names, reads = of_flow(flow, g, parity_there, where)
         return names, [(read, PER) for read in reads]
 
     def of_own(group):
@@ -279,10 +286,10 @@
             (right_of_flow(P_FLOW, g, 1 - parity), entries(t_q, (0, i), theirs[g]))])
         store(q_out, k, i, blocks)
 
-    def p_part(k, i):
+    def p_part(k, i, where=pair):
         g = (0, 1)[k]
-        (blocks,) = products(p_first + i, of_flow(D_FLOW, 0, parity), [
-            (right_of_flow(D_FLOW, g, parity), entries(t_p, (0, i), theirs[(1, 0)[k]]))])
+        (blocks,) = products(p_first + i, of_flow(D_FLOW, 0, parity, where), [
+            (right_of_flow(D_FLOW, g, parity, where), entries(t_p, (0, i), theirs[(1, 0)[k]]))])
         store(p_out, k, i, blocks, fresh=k == 0)
 
     def p_part_q(i):
@@ -372,9 +379,11 @@
     flow_arrived(D_FLOW, 1, 1)
     mirrored(Q_FLOW, 0)
     each_row(p_part_q)
+    near, far = pair[:ROWS], pair[ROWS:]
+    each_row(lambda i: p_part(1, i, near))
     mirrored(D_FLOW, 1)
     for i in range(ROWS):
-        p_part(1, i)
+        p_part(1, i, far)
         send_part(1, 1, i)
     flow_arrived(F_FLOW, 0, 1)
     flow_arrived(F_FLOW, 1, 0)
@@ -403,7 +412,9 @@
         out_specs=pl.BlockSpec(memory_space=pltpu.VMEM),
         scratch_shapes=[
             *[vmem((rows, nz + 1, b, b), f32)] * 2,
-            *[vmem((2, rows, PER + 1, b, b), f32)] * 8,
+            *[vmem((2, rows, PER + 1, b, b), f32)] * 5,
+            *[vmem((rows, PER + 1, b, b), f32)] * 2,
+            *[vmem((2, rows, PER + 1, b, b), f32)] * 2,
             *[vmem((2, rows, PER, b, b), f32)] * 4,
             vmem((rows, nz), i32), *[vmem((2, rows, nz), i32)] * 4,
             *[smem((2, rows, nz), i32)] * 5,

time: 44.6 us -> 44.6 us (level)
  no operation moved by 1% of the time
where the time goes in v10:
time: 44.6 us; the launch traced here: 44.5 us
  Pallas kernels  43.5 us (98%)
  local copies, waits for them, and re-layouts  1.02 us (2%)
    pallas_call x1, Pallas kernels, purified_rows(): pl.pallas_call(purify_kernel, out_shape=jax.ShapeDtypeStruct(density.shap...  43.5 us
    unnamed x1, local copies, waits for them, and re-layouts  1.02 us

profile of v10, /device:TPU:1, one launch (start us, length us, event | category | flops | bytes accessed | tf_op | source)
XLA Modules:
  0.0 44.5 jit_solution(9664792238444242217)
XLA Ops:
  0.0 43.5 %shard_map.28 = f32[2,9,128,128]{3,2,1,0:T(8,128)S(1)} custom-call(f32[2,9,128,128]{3,2,1,0:T(8,128)} %den.1, s32[2,9]{1,0:T(2,128)} %cols.1), custom_call_target="tpu_custom_call" | custom-call | tf_op jit(solution)/shard_map/pallas_call | solution.py:408
  43.5 1.0 %copy.4 = f32[2,9,128,128]{3,2,1,0:T(8,128)} copy(f32[2,9,128,128]{3,2,1,0:T(8,128)S(1)} %shard_map.28) | data formatting | bytes 2359296
